TPU v7x, 128 devices: a whole 4x4x4 slice. The times are simulated.
128 devices in a mesh: chan: 32 (over z, x_lo, y), win: 4 (over x_hi, core).
Axes of the slice: x: 4 (x_hi: 2, x_lo: 2; x = x_hi * 2 + x_lo), y: 4, z: 4, core: 2. Of those that a mesh axis runs over, the one named last changes fastest.
Arguments:
- samples: int32 [6144, 8, 6144], P('chan', 'win'), may hold values from -2048 to 2046
- exponents: int32 [6144, 8, 24], P('chan', 'win'), may hold values from 0 to 4
- alive: int32 [6144], P('chan'), may hold values 0 or 1
- offsets: int32 [128], P('chan'), may hold values from 0 to 191
Outputs:
- stacks: float32 [128, 384, 2048], P('chan', 'win')
All inputs are finite; a program needn't handle non-finite values. No bound on the sum of `alive` on one device may be relied on, other than what follows from the above.
Results may differ from a plain program's by a relative error of at most 0.0032.
Values may be sent and summed in bfloat16 or wider, within the bound.
No kernel may reach another device: no remote copies, remote signals or barrier semaphores. Data moves between devices by JAX's collectives and lax.ppermute only.
A program may use at most 256 MiB of HBM per device.

v0:
```python
import math

import jax
import jax.numpy as jnp
from jax import lax
from jax.sharding import PartitionSpec as P

SEG = 1024
BAND = 192


def passed_along(block, axis, distance):
    devices = range(lax.axis_size(axis))
    route = [(i - distance, i) for i in devices if i - distance in devices]
    return lax.ppermute(block, axis, route)


def block_scale(exponents):
    levels = jnp.arange(5, dtype=jnp.int32)
    powers = jnp.exp2(levels.astype(jnp.float32))
    return jnp.sum(jnp.where(exponents[..., None] == levels, powers, 0.0), axis=-1)


def normalize(samples, exponents, alive):
    channels, windows, length = samples.shape
    block_count = exponents.shape[2]
    amplitude = samples.astype(jnp.float32).reshape(
        channels, windows, block_count, length // block_count
    )
    amplitude = amplitude * block_scale(exponents)[..., None]
    energy = jnp.mean(amplitude * amplitude, axis=(2, 3), keepdims=True)
    factor = alive.astype(jnp.float32)[:, None, None, None] * lax.rsqrt(energy + 1e-06)
    return (amplitude * factor).reshape(channels, windows, length).astype(jnp.bfloat16)


def forward_basis(seg_len):
    full_len = 2 * seg_len
    sample_index = jnp.arange(seg_len, dtype=jnp.int32)
    phases = sample_index[:, None] * sample_index[None, :] % full_len
    angles = phases.astype(jnp.float32) * (2.0 * math.pi / full_len)
    return jnp.concatenate([jnp.cos(angles), -jnp.sin(angles)], axis=1).astype(jnp.bfloat16)


def transform(normed, seg_len):
    channels, windows, length = normed.shape
    seg_count = length // seg_len
    segments = normed.reshape(channels * windows * seg_count, seg_len)
    spectra = jnp.dot(segments, forward_basis(seg_len), preferred_element_type=jnp.float32).astype(
        jnp.bfloat16
    )
    return spectra.reshape(channels, windows * seg_count, 2 * seg_len)


def inverse_table(seg_len, windows, seg_count):
    full_len = 2 * seg_len
    bin_index = jnp.arange(seg_len, dtype=jnp.int32)
    lag_index = jnp.arange(full_len, dtype=jnp.int32) - full_len // 2
    phases = bin_index[:, None] * lag_index[None, :] % full_len
    angles = phases.astype(jnp.float32) * (2.0 * math.pi / full_len)
    weight = jnp.where(bin_index == 0, 1.0, 2.0).astype(jnp.float32) / float(
        full_len * windows * seg_count * seg_len
    )
    return jnp.concatenate(
        [weight[:, None] * jnp.cos(angles), -weight[:, None] * jnp.sin(angles)], axis=0
    )


def widen(local_data):
    lower_parts = [passed_along(local_data, "chan", 1)]
    upper_parts = [passed_along(local_data, "chan", -1)]
    return jnp.concatenate(lower_parts + [local_data] + upper_parts, axis=0)


def shards(samples, exponents, alive, offsets):
    channels, windows, length = samples.shape
    bin_count = SEG
    normed = normalize(samples, exponents, alive)
    extended = widen(transform(normed, SEG))
    sources = jnp.take(extended, offsets + BAND, axis=0)

    def one_band(inputs):
        source, first_row = inputs
        band_rows = lax.dynamic_slice_in_dim(extended, first_row, 2 * BAND, 0)
        src_re = source[:, :bin_count]
        src_im = source[:, bin_count:]
        band_re = band_rows[..., :bin_count]
        band_im = band_rows[..., bin_count:]
        real_part = jnp.einsum("qk,rqk->rk", src_re, band_re, preferred_element_type=jnp.float32)
        real_part = real_part + jnp.einsum(
            "qk,rqk->rk", src_im, band_im, preferred_element_type=jnp.float32
        )
        imag_part = jnp.einsum("qk,rqk->rk", src_re, band_im, preferred_element_type=jnp.float32)
        imag_part = imag_part - jnp.einsum(
            "qk,rqk->rk", src_im, band_re, preferred_element_type=jnp.float32
        )
        return jnp.concatenate([real_part, imag_part], axis=-1)

    cross_terms = lax.map(one_band, (sources, offsets))
    stacked = lax.psum_scatter(cross_terms, "win", scatter_dimension=1, tiled=True)
    lag_table = inverse_table(SEG, windows * lax.axis_size("win"), length // SEG)
    src_count, recv_count, spec_width = stacked.shape
    result = jnp.dot(
        stacked.reshape(src_count * recv_count, spec_width),
        lag_table,
        precision=lax.Precision.HIGHEST,
        preferred_element_type=jnp.float32,
    )
    return result.reshape(src_count, recv_count, 2 * SEG)


def solution(mesh):
    placed = (P("chan", "win", None), P("chan", "win", None), P("chan"), P("chan"))
    return jax.shard_map(
        shards, mesh=mesh, in_specs=placed, out_specs=P("chan", "win", None), check_vma=False
    )
```

profile of v0, /device:TPU:37, one launch (start us, length us, event | category | flops | bytes accessed | tf_op | source)
XLA Modules:
  0.0 633.8 jit_solution(12135277430868044606)
XLA Ops:
  6.5 17.7 %negate_convert_fusion = (bf16[1024,1024]{1,0:T(8,128)(2,1)S(1)}, bf16[1024,1024]{1,0:T(8,128)(2,1)}) fusion(), kind=kLoop, calls=%fused_computation.50 | loop fusion | flops 17825792 | bytes 4194304 | tf_op jit(solution)/shard_map/convert.1
  24.3 0.9 select_reduce_fusion
  25.3 4.3 mul.108
  29.6 12.3 %mul.109 = f32[192,2,6144]{2,1,0:T(2,128)} reshape(f32[192,2,24,256]{3,2,1,0:T(8,128)} %mul.108) | data formatting | bytes 18874368 | tf_op jit(solution)/shard_map/mul | solution.py:30
  41.8 8.8 %multiply_reduce_fusion = f32[192,2]{1,0:T(8,128)S(1)} fusion(f32[192,2,6144]{2,1,0:T(2,128)} %mul.109, s32[192,2,6144]{2,1,0:T(2,128)} %param.6), kind=kLoop, calls=%fused_computation.31 | loop fusion | flops 9436800 | bytes 18875904 | tf_op jit(solution)/shard_map/reduce_sum | solution.py:31
  50.9 9.9 %multiply_convert_fusion = bf16[192,2,6144]{2,1,0:T(2,128)(2,1)} fusion(f32[192,2]{1,0:T(8,128)S(1)} %copy.25, f32[192,2,6144]{2,1,0:T(2,128)} %mul.109, s32[192,2,6144]{2,1,0:T(2,128)} %param.6), kind=kLoop, calls=%fused_computation.30 | loop fusion | flops 9437184 | bytes 23594496 | tf_op jit(solution)/shard_map/convert_element_type | solution.py:33
  60.8 11.2 %reshape.62 = bf16[2304,1024]{1,0:T(8,128)(2,1)} reshape(bf16[192,2,6144]{2,1,0:T(2,128)(2,1)} %multiply_convert_fusion) | data formatting | bytes 9437184 | tf_op jit(solution)/shard_map/reshape | solution.py:47
  72.0 14.6 %convolution_convert_fusion = bf16[2304,2048]{1,0:T(8,128)(2,1)} fusion(bf16[2304,1024]{1,0:T(8,128)(2,1)} %reshape.62, bf16[1024,1024]{1,0:T(8,128)(2,1)S(1)} %get-tuple-element.57, bf16[1024,1024]{1,0:T(8,128)(2,1)} %get-tuple-element.58), kind=kOutput, calls=%fused_computation.29 | convolution fusion | flops 9676783616 | bytes 18350080 | tf_op jit(solution)/shard_map/dot_general | solution.py:48
  86.6 15.1 %reshape.63 = bf16[192,12,2048]{2,1,0:T(8,128)(2,1)} reshape(bf16[2304,2048]{1,0:T(8,128)(2,1)} %convolution_convert_fusion) | data formatting | bytes 18874368 | tf_op jit(solution)/shard_map/reshape | solution.py:51
  101.8 13.4 %copy.26 = bf16[192,12,2048]{2,0,1:T(8,128)(2,1)} copy(bf16[192,12,2048]{2,1,0:T(8,128)(2,1)} %reshape.63) | data formatting | bytes 18874368 | tf_op jit(solution)/shard_map/reshape | solution.py:51
  115.2 3.2 collective-permute-start
  118.4 5.1 collective-permute-start.1
  123.6 200.7 %collective-permute-done = bf16[192,12,2048]{2,0,1:T(8,128)(2,1)} collective-permute-done((bf16[192,12,2048]{2,0,1:T(8,128)(2,1)}, bf16[192,12,2048]{2,0,1:T(8,128)(2,1)}, u32[]{:S(2)}, u32[]{:S(2)}) %collective-permute-start) | collective-permute-done | bytes 9437216 | tf_op jit(solution)/shard_map/ppermute | solution.py:15
  324.2 12.9 %copy_dynamic-update-slice_fusion.1 = bf16[576,12,2048]{2,1,0:T(8,128)(2,1)} fusion(bf16[192,12,2048]{2,0,1:T(8,128)(2,1)} %collective-permute-done), kind=kLoop, calls=%fused_computation.25 | loop fusion | bytes 22020096
  337.1 5.1 constant_dynamic-update-slice_fusion
  342.2 12.9 %copy_dynamic-update-slice_fusion = bf16[576,12,2048]{2,1,0:T(8,128)(2,1)} fusion(bf16[576,12,2048]{2,1,0:T(8,128)(2,1)} %constant_dynamic-update-slice_fusion, bf16[192,12,2048]{2,0,1:T(8,128)(2,1)} %collective-permute-done.1), kind=kLoop, calls=%fused_computation.24 | loop fusion | bytes 22020096 | tf_op jit(solution)/shard_map/concatenate | solution.py:71
  355.1 1.5 gather_fusion
  356.6 140.8 %while.10 = (s32[]{:T(128)}, f32[4,384,2048]{2,1,0:T(8,128)}, s32[4]{0:T(128)S(1)}, bf16[576,12,2048]{2,1,0:T(8,128)(2,1)}, bf16[4,12,2048]{2,1,0:T(8,128)(2,1)S(1)}, /*index=5*/s32[]{:T(128)}, s32[]{:T(128)}, s32[]{:T(128)}, s32[]{}) while((s32[]{:T(128)}, f32[4,384,2048]{2,1,0:T(8,128)}, s32[4]{0:T(128)S(1)}, ...), condition=%wide.region_3.4_spmd, body=%wide.region_2.3_spmd.sunk | while | flops 47210500 | bytes 41239200 | solution.py:98
  359.1 30.0 %fusion.34 = (f32[1024,384]{0,1:T(8,128)S(1)}, f32[1024,384]{0,1:T(8,128)S(1)}, f32[1024,384]{0,1:T(8,128)S(1)}, f32[1024,384]{0,1:T(8,128)S(1)}) fusion(f32[1024,12]{0,1:T(8,128)S(1)} %get-tuple-element.100, bf16[576,12,2048]{2,1,0:T(8,128)(2,1)} %get-tuple-element.129, s32[]{:T(128)S(6)} %select_n.78, s32[]{:T(128)S(6)} %add.101, ...), kind=kLoop, calls=%fused_computation.7.clone.1 | loop fusion | flops 45613056 | bytes 25264136 | tf_op jit(solution)/shard_map/while/body/eval_jaxpr/qk,rqk->rk/dot_general | solution.py:89
  389.2 0.7 subtract_bitcast_fusion.2
  389.8 2.0 fusion.35
  394.3 30.0 %fusion.34 = (f32[1024,384]{0,1:T(8,128)S(1)}, f32[1024,384]{0,1:T(8,128)S(1)}, f32[1024,384]{0,1:T(8,128)S(1)}, f32[1024,384]{0,1:T(8,128)S(1)}) fusion(f32[1024,12]{0,1:T(8,128)S(1)} %get-tuple-element.100, bf16[576,12,2048]{2,1,0:T(8,128)(2,1)} %get-tuple-element.129, s32[]{:T(128)S(6)} %select_n.78, s32[]{:T(128)S(6)} %add.101, ...), kind=kLoop, calls=%fused_computation.7.clone.1 | loop fusion | flops 45613056 | bytes 25264136 | tf_op jit(solution)/shard_map/while/body/eval_jaxpr/qk,rqk->rk/dot_general | solution.py:89
  424.3 0.7 subtract_bitcast_fusion.2
  425.0 2.0 fusion.35
  429.5 30.0 %fusion.34 = (f32[1024,384]{0,1:T(8,128)S(1)}, f32[1024,384]{0,1:T(8,128)S(1)}, f32[1024,384]{0,1:T(8,128)S(1)}, f32[1024,384]{0,1:T(8,128)S(1)}) fusion(f32[1024,12]{0,1:T(8,128)S(1)} %get-tuple-element.100, bf16[576,12,2048]{2,1,0:T(8,128)(2,1)} %get-tuple-element.129, s32[]{:T(128)S(6)} %select_n.78, s32[]{:T(128)S(6)} %add.101, ...), kind=kLoop, calls=%fused_computation.7.clone.1 | loop fusion | flops 45613056 | bytes 25264136 | tf_op jit(solution)/shard_map/while/body/eval_jaxpr/qk,rqk->rk/dot_general | solution.py:89
  459.5 0.7 subtract_bitcast_fusion.2
  460.2 2.1 fusion.35
  464.8 30.0 %fusion.34 = (f32[1024,384]{0,1:T(8,128)S(1)}, f32[1024,384]{0,1:T(8,128)S(1)}, f32[1024,384]{0,1:T(8,128)S(1)}, f32[1024,384]{0,1:T(8,128)S(1)}) fusion(f32[1024,12]{0,1:T(8,128)S(1)} %get-tuple-element.100, bf16[576,12,2048]{2,1,0:T(8,128)(2,1)} %get-tuple-element.129, s32[]{:T(128)S(6)} %select_n.78, s32[]{:T(128)S(6)} %add.101, ...), kind=kLoop, calls=%fused_computation.7.clone.1 | loop fusion | flops 45613056 | bytes 25264136 | tf_op jit(solution)/shard_map/while/body/eval_jaxpr/qk,rqk->rk/dot_general | solution.py:89
  495.4 2.0 fusion.35
  497.5 34.7 %cosine_multiply_fusion = (f32[1024,2048]{1,0:T(8,128)}, f32[1024,2048]{1,0:T(8,128)}) fusion(s32[2048]{0:T(1024)S(1)} %iota_add_fusion, f32[1024]{0:T(1024)S(1)} %get-tuple-element.59, f32[1024]{0:T(1024)S(1)} %get-tuple-element.60), kind=kLoop, calls=%fused_computation.37 | loop fusion | flops 33554432 | bytes 16793600 | tf_op jit(solution)/shard_map/mul | solution.py:64
  532.2 69.7 %reduce-scatter.2.cloned.1.call-done = f32[4,96,2048]{2,1,0:T(8,128)} async-done(((f32[4,384,2048]{2,1,0:T(8,128)}), f32[4,96,2048]{2,1,0:T(8,128)}) %reduce-scatter.2.cloned.1.call-update) | async-done | bytes 3145744 | tf_op jit(solution)/shard_map/reduce_scatter | solution.py:99
  601.9 25.1 %fusion.7 = f32[4,96,2048]{2,1,0:T(8,128)} fusion(f32[4,96,2048]{2,1,0:T(8,128)} %reduce-scatter.2.cloned.1.call-done, f32[1024,2048]{1,0:T(8,128)} %get-tuple-element.56, f32[1024,2048]{1,0:T(8,128)} %get-tuple-element.55), kind=kOutput, calls=%fused_computation.21 | convolution fusion | flops 19331547136 | bytes 23068672 | tf_op jit(solution)/shard_map/dot_general | solution.py:102
  (34 shorter events, 3.7 us)
Async XLA Ops:
  6.5 595.4 %reduce-scatter.2.cloned.1.call-start = ((), (), s32[]{:S(2)}) async-start(), calls=%async_computation.1 | async-start | bytes 15728640 | tf_op jit(solution)/shard_map/reduce_scatter | solution.py:99
  41.8 8.9 %copy-start.1 = (s32[192]{0:T(256)S(1)}, s32[192]{0:T(256)}, u32[]{:S(2)}) copy-start(s32[192]{0:T(256)} %param.8) | copy-start | bytes 2308
  101.8 21.7 %copy-start.2 = (s32[4]{0:T(128)S(1)}, s32[4]{0:T(128)}, u32[]{:S(2)}) copy-start(s32[4]{0:T(128)} %param.9) | copy-start | bytes 52
  115.2 209.0 %collective-permute-start = (bf16[192,12,2048]{2,0,1:T(8,128)(2,1)}, bf16[192,12,2048]{2,0,1:T(8,128)(2,1)}, u32[]{:S(2)}, u32[]{:S(2)}) collective-permute-start(bf16[192,12,2048]{2,0,1:T(8,128)(2,1)} %copy.26), channel_id=1, source_target_pairs={{0,4},{4,8},{8,12},{12,16},{16,20},{20,24},{24,28},{28,32},{32,36}... | collective-permute-start | bytes 28311560 | tf_op jit(solution)/shard_map/ppermute | solution.py:15
  118.4 223.8 %collective-permute-start.1 = (bf16[192,12,2048]{2,0,1:T(8,128)(2,1)}, bf16[192,12,2048]{2,0,1:T(8,128)(2,1)}, u32[]{:S(2)}, u32[]{:S(2)}) collective-permute-start(bf16[192,12,2048]{2,0,1:T(8,128)(2,1)} %copy.26), channel_id=1, source_target_pairs={{4,0},{8,4},{12,8},{16,12},{20,16},{24,20},{28,24},{32,28},{36,32}... | collective-permute-start | bytes 28311560 | tf_op jit(solution)/shard_map/ppermute | solution.py:15
  123.5 213.6 %copy-start = (bf16[192,12,2048]{2,1,0:T(8,128)(2,1)S(1)}, bf16[192,12,2048]{2,1,0:T(8,128)(2,1)}, u32[]{:S(2)}) copy-start(bf16[192,12,2048]{2,1,0:T(8,128)(2,1)} %reshape.63) | copy-start | bytes 28311556
Sparse Core Ops, SparseCore 0:
  497.6 104.2 reduce-scatter.1
where the time goes:
time: 639 us; the launch traced here: 634 us
  waiting for transfers between devices  270 us (42%)
  other arithmetic  203 us (32%)
  local copies, waits for them, and re-layouts  91.5 us (14%)
  matrix products  39.7 us (6%)
  between operations  13.5 us (2%)
  starting transfers between devices  8.28 us (1%)
  loops' own time  7.42 us (1%)
    ppermute x2, waiting for transfers between devices, passed_along(): return lax.ppermute(block, axis, route)  201 us
    dot_general x4, other arithmetic, one_band(): jnp.einsum('qk,rqk->rk', src_im, band_im, preferred_element_type=jnp.floa...  120 us
    reduce_scatter x1, waiting for transfers between devices, shards(): lax.psum_scatter(cross_terms, 'win', scatter_dimension=1, tiled=True)  69.7 us
    mul x1, other arithmetic, inverse_table(): weight[:, None] * jnp.cos(angles)  34.7 us
    reshape x2, local copies, waits for them, and re-layouts, transform(): return spectra.reshape(channels, windows * seg_count, 2 * seg_len)  28.5 us
    dot_general x1, matrix products, shards(): jnp.dot(stacked.reshape(src_count * recv_count, spec_width), lag_table, p...  25.1 us
    unnamed x8, local copies, waits for them, and re-layouts  18 us
    another operation x1, other arithmetic  17.7 us
  transfers between devices with their start and end apart: 3, of which 2 were waited for; matrix products, arithmetic and copies ran while one was open for 8% of the time, Pallas kernels for 0%

commit v1 on v0

v1 whole, which is shorter than its diff:
```python
import math

import jax
import jax.numpy as jnp
import numpy as np
from jax import lax
from jax.experimental import pallas as pl
from jax.experimental.pallas import tpu as pltpu
from jax.sharding import PartitionSpec as P

SEG = 1024
BAND = 192
HALF = 96
CHUNKS = 4
BINS = SEG // CHUNKS
WIDTH = 2 * BINS
FOLD = 32
TILE = 32
SUB = 16
LANES = 128


def small_tables():
    u = np.arange(BINS)
    k = CHUNKS * u[None, :] + np.arange(CHUNKS)[:, None]
    step = np.arange(FOLD)

    def waves(stride):
        phase = (stride * step[None, :, None] * k[:, None, :]) % (2 * SEG)
        angle = phase * (2.0 * math.pi / (2 * SEG))
        return np.concatenate([np.cos(angle), np.sin(angle)], axis=-1).astype(np.float32)

    return waves(FOLD), waves(1)


def table_kernel(coarse_ref, fine_ref, hi_ref, lo_ref):
    fine_cos = fine_ref[0, :, :BINS]
    fine_sin = fine_ref[0, :, BINS:]

    def row_block(a, carry):
        base_cos = coarse_ref[0, pl.ds(a, 1), :BINS]
        base_sin = coarse_ref[0, pl.ds(a, 1), BINS:]
        real = base_cos * fine_cos - base_sin * fine_sin
        imag = -(base_sin * fine_cos + base_cos * fine_sin)
        rows = pl.ds(pl.multiple_of(a * FOLD, FOLD), FOLD)
        for part, lo_lane in ((real, 0), (imag, BINS)):
            top = part.astype(jnp.bfloat16)
            hi_ref[0, rows, lo_lane:lo_lane + BINS] = top
            lo_ref[0, rows, lo_lane:lo_lane + BINS] = (part - top.astype(jnp.float32)).astype(jnp.bfloat16)
        return carry

    lax.fori_loop(0, FOLD, row_block, 0)


def make_tables():
    coarse, fine = small_tables()
    shape = jax.ShapeDtypeStruct((CHUNKS, SEG, WIDTH), jnp.bfloat16)
    small = pl.BlockSpec((1, FOLD, WIDTH), lambda p: (p, 0, 0))
    large = pl.BlockSpec((1, SEG, WIDTH), lambda p: (p, 0, 0))
    return pl.pallas_call(
        table_kernel,
        grid=(CHUNKS,),
        in_specs=[small, small],
        out_specs=[large, large],
        out_shape=[shape, shape],
        name="tables",
    )(jnp.asarray(coarse), jnp.asarray(fine))


def normalize_kernel(half_ref, samples_ref, scale_ref, alive_ref, out_ref, *, seg_count):
    rows_per_channel = samples_ref.shape[0] // TILE
    windows = out_ref.shape[0] // seg_count
    pieces = SEG // LANES
    blocks = scale_ref.shape[1] // windows
    length = seg_count * SEG

    def rows(w, n, piece):
        start = (n * pieces + piece) * windows + w
        return samples_ref[pl.ds(start, TILE, stride=rows_per_channel), :].astype(jnp.float32)

    scale = scale_ref[...]
    for w in range(windows):
        total = jnp.zeros((TILE, LANES), jnp.float32)
        for n in range(seg_count):
            for pair in range(pieces // 2):
                column = w * blocks + n * (pieces // 2) + pair
                first = rows(w, n, 2 * pair)
                second = rows(w, n, 2 * pair + 1)
                weight = scale[:, column:column + 1]
                total = total + (first * first + second * second) * (weight * weight)
        energy = jnp.sum(total, axis=1, keepdims=True) * (1.0 / length)
        factor = alive_ref[...] * lax.rsqrt(energy + 1e-06)
        for n in range(seg_count):
            for pair in range(pieces // 2):
                column = w * blocks + n * (pieces // 2) + pair
                weight = scale[:, column:column + 1] * factor
                for piece in (2 * pair, 2 * pair + 1):
                    value = rows(w, n, piece) * weight
                    out_ref[w * seg_count + n, :, piece * LANES:(piece + 1) * LANES] = value.astype(jnp.bfloat16)


def normalize_half(half, samples_rows, scales, alive, seg_count, windows):
    per_channel = seg_count * (SEG // LANES) * windows
    steps = HALF // TILE
    import functools
    return pl.pallas_call(
        functools.partial(normalize_kernel, seg_count=seg_count),
        grid_spec=pltpu.PrefetchScalarGridSpec(
            num_scalar_prefetch=1,
            grid=(steps,),
            in_specs=[
                pl.BlockSpec((TILE * per_channel, LANES), lambda i, h: (h[0] * steps + i, 0)),
                pl.BlockSpec((TILE, scales.shape[1]), lambda i, h: (h[0] * steps + i, 0)),
                pl.BlockSpec((TILE, 1), lambda i, h: (h[0] * steps + i, 0)),
            ],
            out_specs=pl.BlockSpec((windows * seg_count, TILE, SEG), lambda i, h: (0, i, 0)),
        ),
        out_shape=jax.ShapeDtypeStruct((windows * seg_count, HALF, SEG), jnp.bfloat16),
        name="normalize",
    )(half, samples_rows, scales, alive)


def cross_kernel(limits_ref, near_ref, far_ref, sources_ref, table_ref, own_ref, up_ref, down_ref,
                 band_ref, src_ref, plus_ref, minus_ref):
    step = pl.program_id(0)
    count = near_ref.shape[0]
    seg_total = 2 * count
    table = table_ref[0]

    @pl.when(step == 0)
    def _():
        spec = jnp.dot(sources_ref[...], table, preferred_element_type=jnp.float32)
        spec = spec.astype(jnp.bfloat16).astype(jnp.float32)
        for b in range(BINS // LANES):
            real = spec[:, b * LANES:(b + 1) * LANES]
            imag = spec[:, BINS + b * LANES:BINS + (b + 1) * LANES]
            src_ref[b] = real
            plus_ref[b] = real + imag
            minus_ref[b] = imag - real

    for part, ref in ((0, near_ref), (1, far_ref)):
        rows = ref[...].reshape(count * TILE, SEG)
        spec = jnp.dot(rows, table, preferred_element_type=jnp.float32)
        band_ref[pl.ds(part * count * TILE, count * TILE), :] = spec.astype(jnp.bfloat16).astype(jnp.float32)

    def group(which, out_ref, bank, row):
        lane = pl.multiple_of(bank * LANES, LANES)
        real_lanes = pl.ds(lane, LANES)
        imag_lanes = pl.ds(BINS + lane, LANES)
        zero = jnp.zeros((8, LANES), jnp.float32)
        acc = [[[zero, zero, zero] for _ in range(4)] for _ in range(SUB // 8)]
        for q in range(seg_total):
            band = []
            for t in range(SUB // 8):
                at = pl.ds(q * TILE + row + 8 * t, 8)
                g_re = band_ref[at, real_lanes]
                g_im = band_ref[at, imag_lanes]
                band.append((g_re, g_im, g_re + g_im))
            for j in range(4):
                at = pl.ds((which * 4 + j) * seg_total + q, 8, stride=0)
                s_re = src_ref[bank, at, :]
                s_plus = plus_ref[bank, at, :]
                s_minus = minus_ref[bank, at, :]
                for t in range(SUB // 8):
                    g_re, g_im, g_sum = band[t]
                    a = acc[t][j]
                    a[0] = a[0] + s_re * g_sum
                    a[1] = a[1] + s_minus * g_im
                    a[2] = a[2] + s_plus * g_re
        for j in range(4):
            real = jnp.concatenate([acc[t][j][0] + acc[t][j][1] for t in range(SUB // 8)], axis=0)
            imag = jnp.concatenate([acc[t][j][0] - acc[t][j][2] for t in range(SUB // 8)], axis=0)
            out_ref[j, pl.ds(row, SUB), real_lanes] = real.astype(out_ref.dtype)
            out_ref[j, pl.ds(row, SUB), imag_lanes] = imag.astype(out_ref.dtype)

    def tile(index, carry):
        bank = index % (BINS // LANES)
        row = pl.multiple_of((index // (BINS // LANES)) * SUB, SUB)
        channel = limits_ref[0] + step * TILE + row

        @pl.when(channel + SUB > limits_ref[1])
        def _():
            group(1, up_ref, bank, row)

        @pl.when(channel < limits_ref[2])
        def _():
            group(2, down_ref, bank, row)

        group(0, own_ref, bank, row)
        return carry

    lax.fori_loop(0, (TILE // SUB) * (BINS // LANES), tile, 0)


def cross_chunk(chunk, limits, near, far, sources, tables):
    count = near.shape[0]
    src_rows = sources.shape[0]
    block = pl.BlockSpec((count, TILE, SEG), lambda i, h: (0, i, 0))
    result = pl.BlockSpec((4, TILE, WIDTH), lambda i, h: (0, i, 0))
    return pl.pallas_call(
        cross_kernel,
        grid_spec=pltpu.PrefetchScalarGridSpec(
            num_scalar_prefetch=1,
            grid=(HALF // TILE,),
            in_specs=[
                block,
                block,
                pl.BlockSpec((src_rows, SEG), lambda i, h: (0, 0)),
                pl.BlockSpec((1, SEG, WIDTH), lambda i, h: (chunk, 0, 0)),
            ],
            out_specs=[result, result, result],
            scratch_shapes=[
                pltpu.VMEM((2 * count * TILE, WIDTH), jnp.float32),
                pltpu.VMEM((BINS // LANES, src_rows, LANES), jnp.float32),
                pltpu.VMEM((BINS // LANES, src_rows, LANES), jnp.float32),
                pltpu.VMEM((BINS // LANES, src_rows, LANES), jnp.float32),
            ],
        ),
        out_shape=[
            jax.ShapeDtypeStruct((4, HALF, WIDTH), jnp.float32),
            jax.ShapeDtypeStruct((4, HALF, WIDTH), jnp.bfloat16),
            jax.ShapeDtypeStruct((4, HALF, WIDTH), jnp.bfloat16),
        ],
        name="cross",
    )(limits, near, far, sources, tables)


def inverse_kernel(starts_ref, *refs, chunk):
    if chunk:
        mine_ref, mate_ref, weight_ref, hi_ref, lo_ref, prev_ref, out_ref, top_ref, rest_ref = refs
    else:
        mine_ref, mate_ref, weight_ref, hi_ref, lo_ref, out_ref, top_ref, rest_ref = refs
    source_row = lax.broadcasted_iota(jnp.int32, (HALF, 2 * HALF), 1)
    target_row = lax.broadcasted_iota(jnp.int32, (HALF, 2 * HALF), 0)
    for j in range(4):
        wanted = target_row + starts_ref[j]
        wanted = jnp.where(wanted >= 2 * HALF, wanted - 2 * HALF, wanted)
        turn = jnp.where(source_row == wanted, 1.0, 0.0).astype(jnp.bfloat16)
        rows = jnp.concatenate([mine_ref[j], mate_ref[j]], axis=0) * weight_ref[0]
        top = rows.astype(jnp.bfloat16)
        rest = (rows - top.astype(jnp.float32)).astype(jnp.bfloat16)
        at = pl.ds(j * HALF, HALF)
        top_ref[at, :] = jnp.dot(turn, top, preferred_element_type=jnp.float32).astype(jnp.bfloat16)
        rest_ref[at, :] = jnp.dot(turn, rest, preferred_element_type=jnp.float32).astype(jnp.bfloat16)

    def product(a, b):
        return lax.dot_general(a, b, (((1,), (1,)), ((), ())), preferred_element_type=jnp.float32)

    top = top_ref[...]
    hi = hi_ref[0]
    terms = product(top, hi) + (product(rest_ref[...], hi) + product(top, lo_ref[0]))
    terms = terms.reshape(4, HALF, SEG)
    before = terms if chunk % 2 == 0 else -terms
    if chunk:
        out_ref[:, :, :SEG] = prev_ref[:, :, :SEG] + before
        out_ref[:, :, SEG:] = prev_ref[:, :, SEG:] + terms
    else:
        out_ref[:, :, :SEG] = before
        out_ref[:, :, SEG:] = terms


def inverse_chunk(chunk, starts, mine, mate, weights, hi, lo, prev):
    import functools
    whole = pl.BlockSpec((4, HALF, WIDTH), lambda i, h: (0, 0, 0))
    table = pl.BlockSpec((1, SEG, WIDTH), lambda i, h: (chunk, 0, 0))
    stacks = pl.BlockSpec((4, HALF, 2 * SEG), lambda i, h: (0, 0, 0))
    operands = [starts, mine, mate, weights, hi, lo] + ([prev] if chunk else [])
    return pl.pallas_call(
        functools.partial(inverse_kernel, chunk=chunk),
        grid_spec=pltpu.PrefetchScalarGridSpec(
            num_scalar_prefetch=1,
            grid=(1,),
            in_specs=[whole, whole, pl.BlockSpec((1, 1, WIDTH), lambda i, h: (chunk, 0, 0)), table, table]
            + ([stacks] if chunk else []),
            out_specs=stacks,
            scratch_shapes=[
                pltpu.VMEM((4 * HALF, WIDTH), jnp.bfloat16),
                pltpu.VMEM((4 * HALF, WIDTH), jnp.bfloat16),
            ],
        ),
        out_shape=jax.ShapeDtypeStruct((4, HALF, 2 * SEG), jnp.float32),
        input_output_aliases={6: 0} if chunk else {},
        name="inverse",
    )(*operands)


def block_scale(exponents):
    levels = jnp.arange(5, dtype=jnp.int32)
    powers = jnp.exp2(levels.astype(jnp.float32))
    return jnp.sum(jnp.where(exponents[..., None] == levels, powers, 0.0), axis=-1)


def passed_along(block, axis, distance):
    devices = range(lax.axis_size(axis))
    route = [(i - distance, i) for i in devices if i - distance in devices]
    return lax.ppermute(block, axis, route)


def partner(block, bit):
    return lax.ppermute(block, "win", [(i, i ^ bit) for i in range(lax.axis_size("win"))])


def source_rows(samples_rows, scales, alive, offsets, windows, seg_count):
    pieces = SEG // LANES
    blocks = seg_count * pieces // 2
    per_channel = seg_count * pieces * windows
    values, factors, lives = [], [], []
    for j in range(4):
        values.append(lax.dynamic_slice_in_dim(samples_rows, offsets[j] * per_channel, per_channel, 0))
        factors.append(lax.dynamic_slice_in_dim(scales, offsets[j], 1, 0))
        lives.append(lax.dynamic_slice_in_dim(alive, offsets[j], 1, 0))
    raw = jnp.stack(values).astype(jnp.float32).reshape(4, blocks, 2, windows, LANES)
    scale = jnp.concatenate(factors).reshape(4, windows, blocks).transpose(0, 2, 1)
    amplitude = raw * scale[:, :, None, :, None]
    energy = jnp.mean(amplitude * amplitude, axis=(1, 2, 4), keepdims=True)
    factor = jnp.concatenate(lives).reshape(4, 1, 1, 1, 1) * lax.rsqrt(energy + 1e-06)
    normed = (amplitude * factor).astype(jnp.bfloat16)
    normed = normed.reshape(4, seg_count, pieces, windows, LANES).transpose(0, 3, 1, 2, 4)
    return normed.reshape(4, windows * seg_count, SEG)


def shards(samples, exponents, alive, offsets):
    channels, windows, length = samples.shape
    seg_count = length // SEG
    place = lax.axis_index("win")
    chan = lax.axis_index("chan")
    core = place % 2
    upper_half = place // 2
    last = lax.axis_size("chan") - 1

    samples_rows = samples.reshape(channels, windows, length // LANES, LANES)
    samples_rows = samples_rows.transpose(0, 2, 1, 3).reshape(channels * windows * (length // LANES), LANES)
    scales = block_scale(exponents).reshape(channels, -1)
    live = alive.astype(jnp.float32).reshape(channels, 1)

    own_src = source_rows(samples_rows, scales, live, offsets, windows, seg_count)
    own_src = jnp.concatenate([own_src, partner(own_src, 1)], axis=1)
    above_src = passed_along(own_src, "chan", -1)
    below_src = passed_along(own_src, "chan", 1)
    above_off = passed_along(offsets, "chan", -1)
    below_off = passed_along(offsets, "chan", 1)
    sources = jnp.concatenate([own_src, above_src, below_src], axis=0).reshape(-1, SEG)
    lowest = jnp.where(chan == last, channels, jnp.min(above_off))
    highest = jnp.where(chan == 0, 0, jnp.max(below_off))
    limits = jnp.stack([core * HALF, lowest, highest]).astype(jnp.int32)

    sent = normalize_half((1 - core).reshape(1), samples_rows, scales, live, seg_count, windows)
    far = partner(sent, 1)
    near = normalize_half(core.reshape(1), samples_rows, scales, live, seg_count, windows)
    hi, lo = make_tables()

    index = core * HALF + jnp.arange(HALF, dtype=jnp.int32)
    below_source = (index[None, :] < offsets[:, None])[:, :, None]
    keep_own = below_source == (upper_half == 0)
    k = CHUNKS * np.arange(BINS)[None, :] + np.arange(CHUNKS)[:, None]
    weights = np.where(k == 0, 1.0, 2.0) / float(2 * SEG * windows * 4 * seg_count * SEG)
    weights = jnp.asarray(np.concatenate([weights, weights], axis=1).astype(np.float32).reshape(CHUNKS, 1, WIDTH))

    stacks = None
    for chunk in range(CHUNKS):
        own, to_above, to_below = cross_chunk(chunk, limits, near, far, sources, hi)
        from_below = passed_along(to_above, "chan", 1)
        from_above = passed_along(to_below, "chan", -1)
        other = jnp.where(below_source, from_above, from_below).astype(jnp.float32)
        kept = jnp.where(keep_own, own, other)
        passed = jnp.where(keep_own, other, own).astype(jnp.bfloat16)
        total = kept + partner(passed, 2).astype(jnp.float32)
        mate = partner(total, 1)
        stacks = inverse_chunk(chunk, offsets, total, mate, weights, hi, lo, stacks)
    return stacks


def solution(mesh):
    placed = (P("chan", "win", None), P("chan", "win", None), P("chan"), P("chan"))
    return jax.shard_map(
        shards, mesh=mesh, in_specs=placed, out_specs=P("chan", "win", None), check_vma=False
    )
```

time: 639 us -> 259 us (0.41)
  waiting for transfers between devices: 270 us -> 41.3 us
  other arithmetic: 203 us -> 12.3 us
  Pallas kernels: 0 us -> 124 us
  local copies, waits for them, and re-layouts: 91.5 us -> 9.37 us
  starting transfers between devices: 8.28 us -> 57.8 us
  matrix products: 39.7 us -> 0 us
  loops' own time: 7.42 us -> 0 us
    ppermute x2 -> x12, waiting for transfers between devices: 201 us -> 11.1 us  [passed_along(): return lax.ppermute(block, axis, route)]
    pallas_call x0 -> x11, Pallas kernels: none -> 124 us  [the longest x4 60.9 us: cross_chunk(): pl.pallas_call(cross_kernel, grid_spec=pltpu.PrefetchScalarGridSpec(num_s...]
    dot_general x4 -> x0, other arithmetic: 120 us -> none  [one_band(): jnp.einsum('qk,rqk->rk', src_im, band_im, preferred_element_type=jnp.floa...]
    reduce_scatter x1 -> x0, waiting for transfers between devices: 69.7 us -> none  [shards(): lax.psum_scatter(cross_terms, 'win', scatter_dimension=1, tiled=True)]
    dot_general x2 -> x0, matrix products: 39.7 us -> none  [the longest x1 25.1 us: shards(): jnp.dot(stacked.reshape(src_count * recv_count, spec_width), lag_table, p...]
    reshape x3 -> x4, local copies, waits for them, and re-layouts: 39.8 us -> 1.6 us  [the longest x1 0.75 us: shards(): live = alive.astype(jnp.float32).reshape(channels, 1)]
    ppermute x2 -> x12, starting transfers between devices: 8.28 us -> 45.6 us  [passed_along(): return lax.ppermute(block, axis, route)]
    mul x2, other arithmetic: 34.7 us -> 2.66 us  [source_rows(): jnp.concatenate(lives).reshape(4, 1, 1, 1, 1) * lax.rsqrt(energy + 1e-06)]
  transfers between devices with their start and end apart: 3 -> 22, of which waited for: 2 -> 9; matrix products, arithmetic and copies ran while one was open for 8% -> 4% of each run, Pallas kernels for 0% -> 34%
where the time goes in v1:
time: 259 us; the launch traced here: 256 us
  Pallas kernels  124 us (48%)
  starting transfers between devices  57.8 us (22%)
  waiting for transfers between devices  41.3 us (16%)
  other arithmetic  12.3 us (5%)
  between operations  11.9 us (5%)
  local copies, waits for them, and re-layouts  9.37 us (4%)
    pallas_call x4, Pallas kernels, cross_chunk(): pl.pallas_call(cross_kernel, grid_spec=pltpu.PrefetchScalarGridSpec(num_s...  60.9 us
    ppermute x12, starting transfers between devices, passed_along(): return lax.ppermute(block, axis, route)  45.6 us
    ppermute x10, waiting for transfers between devices, partner(): lax.ppermute(block, 'win', [(i, i ^ bit) for i in range(lax.axis_size('wi...  30.2 us
    pallas_call x2, Pallas kernels, normalize_half(): pl.pallas_call(functools.partial(normalize_kernel, seg_count=seg_count),...  29.3 us
    pallas_call x4, Pallas kernels, inverse_chunk(): pl.pallas_call(functools.partial(inverse_kernel, chunk=chunk), grid_spec=...  27.6 us
    ppermute x10, starting transfers between devices, partner(): lax.ppermute(block, 'win', [(i, i ^ bit) for i in range(lax.axis_size('wi...  12.2 us
    ppermute x12, waiting for transfers between devices, passed_along(): return lax.ppermute(block, axis, route)  11.1 us
    pallas_call x1, Pallas kernels, make_tables(): pl.pallas_call(table_kernel, grid=(CHUNKS,), in_specs=[small, small], out...  6.03 us
  transfers between devices with their start and end apart: 22, of which 9 were waited for; matrix products, arithmetic and copies ran while one was open for 4% of the time, Pallas kernels for 34%

profile of v1, /device:TPU:37, one launch (start us, length us, event | category | flops | bytes accessed | tf_op | source)
XLA Modules:
  0.0 256.4 jit_solution(480418515094431661)
XLA Ops:
  3.1 14.7 %normalize.3 = bf16[12,96,1024]{2,1,0:T(8,128)(2,1)} custom-call(s32[1]{0:T(128)} %bitcast.9.half_ref, s32[18432,128]{1,0:T(8,128)} %bitcast.39, f32[192,48]{1,0:T(8,128)} %copy.40.scale_ref, f32[192,1]{1,0:T(8,128)} %copy.41.alive_ref), custom_call_target="tpu_custom_call" | custom-call | tf_op jit(solution)/shard_map/normalize/pallas_call | solution.py:106
  31.1 2.6 %maximum_bitcast_fusion = f32[4]{0:T(128)S(1)} fusion(f32[1,1]{0,1:T(1,128)} %bitcast.25, f32[1,1]{0,1:T(1,128)} %bitcast.24, f32[1,1]{0,1:T(1,128)} %bitcast.23, f32[1,1]{0,1:T(1,128)} %bitcast.22), kind=kLoop, calls=%fused_computation.47 | loop fusion | flops 12 | bytes 32 | tf_op jit(solution)/shard_map/mul | solution.py:316
  36.7 3.2 %collective-permute-start.5 = (bf16[4,24,1024]{2,0,1:T(4,128)(2,1)S(1)}, bf16[4,24,1024]{2,0,1:T(4,128)(2,1)S(1)}, u32[]{:S(2)}, u32[]{:S(2)}) collective-permute-start(bf16[4,24,1024]{2,0,1:T(4,128)(2,1)S(1)} %constant_dynamic-update-slice_fusion), channel_id=1, source_target_pairs={{0,4},{4,8},{8,12},{12,16},{16,20},{20,24},{24,28},{28,32},{32,36}... | collective-permute-start | bytes 589832 | tf_op jit(solution)/shard_map/ppermute | solution.py:296
  39.9 5.1 %collective-permute-start.4 = (bf16[4,24,1024]{2,0,1:T(4,128)(2,1)S(1)}, bf16[4,24,1024]{2,0,1:T(4,128)(2,1)S(1)}, u32[]{:S(2)}, u32[]{:S(2)}) collective-permute-start(bf16[4,24,1024]{2,0,1:T(4,128)(2,1)S(1)} %constant_dynamic-update-slice_fusion), channel_id=1, source_target_pairs={{4,0},{8,4},{12,8},{16,12},{20,16},{24,20},{28,24},{32,28},{36,32}... | collective-permute-start | bytes 589832 | tf_op jit(solution)/shard_map/ppermute | solution.py:296
  46.9 6.4 %collective-permute-start = (s32[4]{0:T(128)S(1)}, s32[4]{0:T(128)S(1)}, u32[]{:S(2)}, u32[]{:S(2)}) collective-permute-start(s32[4]{0:T(128)S(1)} %copy-done.15), channel_id=1, source_target_pairs={{4,0},{8,4},{12,8},{16,12},{20,16},{24,20},{28,24},{32,28},{36,32}... | collective-permute-start | bytes 56 | tf_op jit(solution)/shard_map/ppermute | solution.py:296
  53.3 14.6 %normalize.2.near_ref = bf16[12,96,1024]{2,1,0:T(8,128)(2,1)} custom-call(s32[1]{0:T(128)} %bitcast.3.half_ref, s32[18432,128]{1,0:T(8,128)} %bitcast.41, f32[192,48]{1,0:T(8,128)} %copy.40.scale_ref, f32[192,1]{1,0:T(8,128)} %copy.41.alive_ref), custom_call_target="tpu_custom_call" | custom-call | tf_op jit(solution)/shard_map/normalize/pallas_call | solution.py:106
  67.9 6.0 %tables.1 = (bf16[4,1024,512]{2,1,0:T(8,128)(2,1)}, bf16[4,1024,512]{2,1,0:T(8,128)(2,1)}) custom-call(f32[4,32,512]{2,1,0:T(8,128)} %constant.62.clone.coarse_ref, f32[4,32,512]{2,1,0:T(8,128)} %constant.63.clone.fine_ref), custom_call_target="tpu_custom_call" | custom-call | tf_op jit(solution)/shard_map/tables/pallas_call | solution.py:60
  80.3 15.3 %cross.7 = (f32[4,96,512]{2,1,0:T(8,128)}, bf16[4,96,512]{2,1,0:T(8,128)(2,1)}, bf16[4,96,512]{2,1,0:T(8,128)(2,1)}) custom-call(s32[3]{0:T(128)} %pad_add_fusion.limits_ref, bf16[12,96,1024]{2,1,0:T(8,128)(2,1)} %normalize.2.near_ref, bf16[12,96,1024]{2,1,0:T(8,128)(2,1)} %copy-done, bf16[288,1024]{1,0:T(8,128)(2,1)} %bitcast.42, ...), custom_call_target="tpu_custom_call" | custom-call | tf_op jit(solution)/shard_map/cross/pallas_call | solution.py:200
  97.5 3.4 %collective-permute-start.19 = (bf16[4,96,512]{2,1,0:T(8,128)(2,1)}, bf16[4,96,512]{2,1,0:T(8,128)(2,1)S(1)}, u32[]{:S(2)}, u32[]{:S(2)}) collective-permute-start(bf16[4,96,512]{2,1,0:T(8,128)(2,1)} %get-tuple-element.32), channel_id=1, source_target_pairs={{0,4},{4,8},{8,12},{12,16},{16,20},{20,24},{24,28},{28,32},{32,36}... | collective-permute-start | bytes 1179656 | tf_op jit(solution)/shard_map/ppermute | solution.py:296
  100.9 15.2 %cross.6 = (f32[4,96,512]{2,1,0:T(8,128)}, bf16[4,96,512]{2,1,0:T(8,128)(2,1)}, bf16[4,96,512]{2,1,0:T(8,128)(2,1)}) custom-call(s32[3]{0:T(128)} %pad_add_fusion.limits_ref, bf16[12,96,1024]{2,1,0:T(8,128)(2,1)} %normalize.2.near_ref, bf16[12,96,1024]{2,1,0:T(8,128)(2,1)} %copy-done, bf16[288,1024]{1,0:T(8,128)(2,1)} %bitcast.43, ...), custom_call_target="tpu_custom_call" | custom-call | tf_op jit(solution)/shard_map/cross/pallas_call | solution.py:200
  116.1 4.9 %collective-permute-start.14 = (bf16[4,96,512]{2,1,0:T(8,128)(2,1)}, bf16[4,96,512]{2,1,0:T(8,128)(2,1)S(1)}, u32[]{:S(2)}, u32[]{:S(2)}) collective-permute-start(bf16[4,96,512]{2,1,0:T(8,128)(2,1)} %get-tuple-element.28), channel_id=1, source_target_pairs={{4,0},{8,4},{12,8},{16,12},{20,16},{24,20},{28,24},{32,28},{36,32}... | collective-permute-start | bytes 1179656 | tf_op jit(solution)/shard_map/ppermute | solution.py:296
  121.0 2.1 collective-permute-start.15
  123.1 15.2 %cross.5 = (f32[4,96,512]{2,1,0:T(8,128)}, bf16[4,96,512]{2,1,0:T(8,128)(2,1)}, bf16[4,96,512]{2,1,0:T(8,128)(2,1)}) custom-call(s32[3]{0:T(128)} %pad_add_fusion.limits_ref, bf16[12,96,1024]{2,1,0:T(8,128)(2,1)} %normalize.2.near_ref, bf16[12,96,1024]{2,1,0:T(8,128)(2,1)} %copy-done, bf16[288,1024]{1,0:T(8,128)(2,1)} %bitcast.44, ...), custom_call_target="tpu_custom_call" | custom-call | tf_op jit(solution)/shard_map/cross/pallas_call | solution.py:200
  138.3 6.5 %collective-permute-start.10 = (bf16[4,96,512]{2,1,0:T(8,128)(2,1)}, bf16[4,96,512]{2,1,0:T(8,128)(2,1)}, u32[]{:S(2)}, u32[]{:S(2)}) collective-permute-start(bf16[4,96,512]{2,1,0:T(8,128)(2,1)} %get-tuple-element.25), channel_id=1, source_target_pairs={{4,0},{8,4},{12,8},{16,12},{20,16},{24,20},{28,24},{32,28},{36,32}... | collective-permute-start | bytes 1179656 | tf_op jit(solution)/shard_map/ppermute | solution.py:296
  144.8 15.2 %cross.4 = (f32[4,96,512]{2,1,0:T(8,128)}, bf16[4,96,512]{2,1,0:T(8,128)(2,1)}, bf16[4,96,512]{2,1,0:T(8,128)(2,1)}) custom-call(s32[3]{0:T(128)} %pad_add_fusion.limits_ref, bf16[12,96,1024]{2,1,0:T(8,128)(2,1)} %normalize.2.near_ref, bf16[12,96,1024]{2,1,0:T(8,128)(2,1)} %copy-done, bf16[288,1024]{1,0:T(8,128)(2,1)} %bitcast.45, ...), custom_call_target="tpu_custom_call" | custom-call | tf_op jit(solution)/shard_map/cross/pallas_call | solution.py:200
  162.0 6.4 %collective-permute-start.6 = (bf16[4,96,512]{2,1,0:T(8,128)(2,1)}, bf16[4,96,512]{2,1,0:T(8,128)(2,1)}, u32[]{:S(2)}, u32[]{:S(2)}) collective-permute-start(bf16[4,96,512]{2,1,0:T(8,128)(2,1)} %get-tuple-element.21), channel_id=1, source_target_pairs={{4,0},{8,4},{12,8},{16,12},{20,16},{24,20},{28,24},{32,28},{36,32}... | collective-permute-start | bytes 1179656 | tf_op jit(solution)/shard_map/ppermute | solution.py:296
  168.4 1.9 collective-permute-start.7
  170.5 3.1 %collective-permute-done.11 = bf16[4,96,512]{2,1,0:T(8,128)(2,1)} collective-permute-done((bf16[4,96,512]{2,1,0:T(8,128)(2,1)}, bf16[4,96,512]{2,1,0:T(8,128)(2,1)}, u32[]{:S(2)}, u32[]{:S(2)}) %collective-permute-start.11) | collective-permute-done | bytes 393248 | tf_op jit(solution)/shard_map/ppermute | solution.py:296
  174.5 7.0 %collective-permute-done.7 = bf16[4,96,512]{2,1,0:T(8,128)(2,1)} collective-permute-done((bf16[4,96,512]{2,1,0:T(8,128)(2,1)}, bf16[4,96,512]{2,1,0:T(8,128)(2,1)}, u32[]{:S(2)}, u32[]{:S(2)}) %collective-permute-start.7) | collective-permute-done | bytes 393248 | tf_op jit(solution)/shard_map/ppermute | solution.py:296
  181.5 2.4 fusion.7
  184.3 2.7 %collective-permute-start.8 = (bf16[4,96,512]{2,1,0:T(8,128)(2,1)S(1)}, bf16[4,96,512]{2,1,0:T(8,128)(2,1)S(1)}, u32[]{:S(2)}, u32[]{:S(2)}) collective-permute-start(bf16[4,96,512]{2,1,0:T(8,128)(2,1)S(1)} %get-tuple-element.48), channel_id=1, source_target_pairs={{0,2},{1,3},{2,0},{3,1},{4,6},{5,7},{6,4},{7,5},{8,10},{9,11},{10,... | collective-permute-start | bytes 1179656 | tf_op jit(solution)/shard_map/ppermute | solution.py:300
  187.3 2.7 %collective-permute-start.16 = (bf16[4,96,512]{2,1,0:T(8,128)(2,1)S(1)}, bf16[4,96,512]{2,1,0:T(8,128)(2,1)S(1)}, u32[]{:S(2)}, u32[]{:S(2)}) collective-permute-start(bf16[4,96,512]{2,1,0:T(8,128)(2,1)S(1)} %get-tuple-element.50), channel_id=1, source_target_pairs={{0,2},{1,3},{2,0},{3,1},{4,6},{5,7},{6,4},{7,5},{8,10},{9,11},{10,... | collective-permute-start | bytes 1179656 | tf_op jit(solution)/shard_map/ppermute | solution.py:300
  190.0 2.5 collective-permute-done.20
  192.5 8.4 %collective-permute-done.8 = bf16[4,96,512]{2,1,0:T(8,128)(2,1)S(1)} collective-permute-done((bf16[4,96,512]{2,1,0:T(8,128)(2,1)S(1)}, bf16[4,96,512]{2,1,0:T(8,128)(2,1)S(1)}, u32[]{:S(2)}, u32[]{:S(2)}) %collective-permute-start.8) | collective-permute-done | bytes 393248 | tf_op jit(solution)/shard_map/ppermute | solution.py:300
  201.0 8.4 %collective-permute-done.12 = bf16[4,96,512]{2,1,0:T(8,128)(2,1)S(1)} collective-permute-done((bf16[4,96,512]{2,1,0:T(8,128)(2,1)S(1)}, bf16[4,96,512]{2,1,0:T(8,128)(2,1)S(1)}, u32[]{:S(2)}, u32[]{:S(2)}) %collective-permute-start.12) | collective-permute-done | bytes 393248 | tf_op jit(solution)/shard_map/ppermute | solution.py:300
  209.4 8.4 %collective-permute-done.16 = bf16[4,96,512]{2,1,0:T(8,128)(2,1)S(1)} collective-permute-done((bf16[4,96,512]{2,1,0:T(8,128)(2,1)S(1)}, bf16[4,96,512]{2,1,0:T(8,128)(2,1)S(1)}, u32[]{:S(2)}, u32[]{:S(2)}) %collective-permute-start.16) | collective-permute-done | bytes 393248 | tf_op jit(solution)/shard_map/ppermute | solution.py:300
  217.8 2.5 fusion.6
  220.4 4.7 %collective-permute-start.21 = (f32[4,96,512]{2,1,0:T(8,128)S(1)}, f32[4,96,512]{2,1,0:T(8,128)S(1)}, u32[]{:S(2)}, u32[]{:S(2)}) collective-permute-start(f32[4,96,512]{2,1,0:T(8,128)S(1)} %get-tuple-element.43.refs_0_), channel_id=1, source_target_pairs={{0,1},{1,0},{2,3},{3,2},{4,5},{5,4},{6,7},{7,6},{8,9},{9,8},{10,11... | collective-permute-start | bytes 2359304 | tf_op jit(solution)/shard_map/ppermute | solution.py:300
  227.9 6.1 %inverse.4.refs_5_ = f32[4,96,2048]{2,1,0:T(8,128)} custom-call(s32[4]{0:T(128)} %starts_ref.7, f32[4,96,512]{2,1,0:T(8,128)} %copy-done.10, f32[4,96,512]{2,1,0:T(8,128)} %copy-done.14, f32[4,1,512]{2,1,0:T(1,128)} %constant.64.clone.refs_2_, bf16[4,1024,512]{2,1,0:T(8,128)(2,1)} %get-tuple-element.19.table_ref.refs_3_, ...), custom_call_target="tpu_custom_call" | custom-call | tf_op jit(solution)/shard_map/inverse/pallas_call | solution.py:268
  234.0 7.2 %inverse.5.refs_5_ = f32[4,96,2048]{2,1,0:T(8,128)} custom-call(s32[4]{0:T(128)} %starts_ref.7, f32[4,96,512]{2,1,0:T(8,128)} %copy-done.3, f32[4,96,512]{2,1,0:T(8,128)} %collective-permute-done.17.refs_1_, f32[4,1,512]{2,1,0:T(1,128)} %constant.64.clone.refs_2_, ...), custom_call_target="tpu_custom_call", output_to_operand_aliasing={{}: (6, {})} | custom-call | tf_op jit(solution)/shard_map/inverse/pallas_call | solution.py:268
  241.2 7.2 %inverse.6.refs_5_ = f32[4,96,2048]{2,1,0:T(8,128)} custom-call(s32[4]{0:T(128)} %starts_ref.7, f32[4,96,512]{2,1,0:T(8,128)} %copy-done.2, f32[4,96,512]{2,1,0:T(8,128)} %collective-permute-done.13.refs_1_, f32[4,1,512]{2,1,0:T(1,128)} %constant.64.clone.refs_2_, ...), custom_call_target="tpu_custom_call", output_to_operand_aliasing={{}: (6, {})} | custom-call | tf_op jit(solution)/shard_map/inverse/pallas_call | solution.py:268
  249.2 7.2 %inverse.7 = f32[4,96,2048]{2,1,0:T(8,128)} custom-call(s32[4]{0:T(128)} %starts_ref.7, f32[4,96,512]{2,1,0:T(8,128)} %copy-done.1, f32[4,96,512]{2,1,0:T(8,128)} %copy-done.13, f32[4,1,512]{2,1,0:T(1,128)} %constant.64.clone.refs_2_, bf16[4,1024,512]{2,1,0:T(8,128)(2,1)} %get-tuple-element.19.table_ref.refs_3_, ...), custom_call_target="tpu_custom_call", output_to_operand_aliasing={{}: (6, {})} | custom-call | tf_op jit(solution)/shard_map/inverse/pallas_call | solution.py:268
  (91 shorter events, 25.2 us)
Async XLA Ops:
  3.1 15.4 %copy-start.15 = (s32[4]{0:T(128)S(1)}, s32[4]{0:T(128)}, u32[]{:S(2)}) copy-start(s32[4]{0:T(128)} %starts_ref.7) | copy-start | bytes 52
  17.8 61.1 %collective-permute-start.2 = (bf16[12,96,1024]{2,1,0:T(8,128)(2,1)}, bf16[12,96,1024]{2,1,0:T(8,128)(2,1)S(1)}, u32[]{:S(2)}, u32[]{:S(2)}) collective-permute-start(bf16[12,96,1024]{2,1,0:T(8,128)(2,1)} %normalize.3), channel_id=1, source_target_pairs={{0,1},{1,0},{2,3},{3,2},{4,5},{5,4},{6,7},{7,6},{8,9},{9,8},{10,11... | collective-permute-start | bytes 7077896 | tf_op jit(solution)/shard_map/ppermute | solution.py:300
  35.3 1.4 collective-permute-start.3
  36.7 40.7 %collective-permute-start.5 = (bf16[4,24,1024]{2,0,1:T(4,128)(2,1)S(1)}, bf16[4,24,1024]{2,0,1:T(4,128)(2,1)S(1)}, u32[]{:S(2)}, u32[]{:S(2)}) collective-permute-start(bf16[4,24,1024]{2,0,1:T(4,128)(2,1)S(1)} %constant_dynamic-update-slice_fusion), channel_id=1, source_target_pairs={{0,4},{4,8},{8,12},{12,16},{16,20},{20,24},{24,28},{28,32},{32,36}... | collective-permute-start | bytes 589832 | tf_op jit(solution)/shard_map/ppermute | solution.py:296
  39.9 37.5 %collective-permute-start.4 = (bf16[4,24,1024]{2,0,1:T(4,128)(2,1)S(1)}, bf16[4,24,1024]{2,0,1:T(4,128)(2,1)S(1)}, u32[]{:S(2)}, u32[]{:S(2)}) collective-permute-start(bf16[4,24,1024]{2,0,1:T(4,128)(2,1)S(1)} %constant_dynamic-update-slice_fusion), channel_id=1, source_target_pairs={{4,0},{8,4},{12,8},{16,12},{20,16},{24,20},{28,24},{32,28},{36,32}... | collective-permute-start | bytes 589832 | tf_op jit(solution)/shard_map/ppermute | solution.py:296
  45.0 29.0 %collective-permute-start.1 = (s32[4]{0:T(128)S(1)}, s32[4]{0:T(128)S(1)}, u32[]{:S(2)}, u32[]{:S(2)}) collective-permute-start(s32[4]{0:T(128)S(1)} %copy-done.15), channel_id=1, source_target_pairs={{0,4},{4,8},{8,12},{12,16},{16,20},{20,24},{24,28},{28,32},{32,36}... | collective-permute-start | bytes 56 | tf_op jit(solution)/shard_map/ppermute | solution.py:296
  46.9 28.4 %collective-permute-start = (s32[4]{0:T(128)S(1)}, s32[4]{0:T(128)S(1)}, u32[]{:S(2)}, u32[]{:S(2)}) collective-permute-start(s32[4]{0:T(128)S(1)} %copy-done.15), channel_id=1, source_target_pairs={{4,0},{8,4},{12,8},{16,12},{20,16},{24,20},{28,24},{32,28},{36,32}... | collective-permute-start | bytes 56 | tf_op jit(solution)/shard_map/ppermute | solution.py:296
  95.6 64.5 %collective-permute-start.18 = (bf16[4,96,512]{2,1,0:T(8,128)(2,1)}, bf16[4,96,512]{2,1,0:T(8,128)(2,1)S(1)}, u32[]{:S(2)}, u32[]{:S(2)}) collective-permute-start(bf16[4,96,512]{2,1,0:T(8,128)(2,1)} %get-tuple-element.31), channel_id=1, source_target_pairs={{4,0},{8,4},{12,8},{16,12},{20,16},{24,20},{28,24},{32,28},{36,32}... | collective-permute-start | bytes 1179656 | tf_op jit(solution)/shard_map/ppermute | solution.py:296
  97.5 64.5 %collective-permute-start.19 = (bf16[4,96,512]{2,1,0:T(8,128)(2,1)}, bf16[4,96,512]{2,1,0:T(8,128)(2,1)S(1)}, u32[]{:S(2)}, u32[]{:S(2)}) collective-permute-start(bf16[4,96,512]{2,1,0:T(8,128)(2,1)} %get-tuple-element.32), channel_id=1, source_target_pairs={{0,4},{4,8},{8,12},{12,16},{16,20},{20,24},{24,28},{28,32},{32,36}... | collective-permute-start | bytes 1179656 | tf_op jit(solution)/shard_map/ppermute | solution.py:296
  116.1 52.3 %collective-permute-start.14 = (bf16[4,96,512]{2,1,0:T(8,128)(2,1)}, bf16[4,96,512]{2,1,0:T(8,128)(2,1)S(1)}, u32[]{:S(2)}, u32[]{:S(2)}) collective-permute-start(bf16[4,96,512]{2,1,0:T(8,128)(2,1)} %get-tuple-element.28), channel_id=1, source_target_pairs={{4,0},{8,4},{12,8},{16,12},{20,16},{24,20},{28,24},{32,28},{36,32}... | collective-permute-start | bytes 1179656 | tf_op jit(solution)/shard_map/ppermute | solution.py:296
  121.0 49.5 %collective-permute-start.15 = (bf16[4,96,512]{2,1,0:T(8,128)(2,1)}, bf16[4,96,512]{2,1,0:T(8,128)(2,1)}, u32[]{:S(2)}, u32[]{:S(2)}) collective-permute-start(bf16[4,96,512]{2,1,0:T(8,128)(2,1)} %get-tuple-element.29), channel_id=1, source_target_pairs={{0,4},{4,8},{8,12},{12,16},{16,20},{20,24},{24,28},{28,32},{32,36}... | collective-permute-start | bytes 1179656 | tf_op jit(solution)/shard_map/ppermute | solution.py:296
  138.3 43.2 %copy-start.4 = (f32[4,96,512]{2,1,0:T(8,128)S(1)}, f32[4,96,512]{2,1,0:T(8,128)}, u32[]{:S(2)}) copy-start(f32[4,96,512]{2,1,0:T(8,128)} %get-tuple-element.30) | copy-start | bytes 2359300
  138.3 43.2 %copy-start.5 = (f32[4,96,512]{2,1,0:T(8,128)S(1)}, f32[4,96,512]{2,1,0:T(8,128)}, u32[]{:S(2)}) copy-start(f32[4,96,512]{2,1,0:T(8,128)} %get-tuple-element.27) | copy-start | bytes 2359300
  138.3 43.2 %copy-start.7 = (f32[4,96,512]{2,1,0:T(8,128)S(1)}, f32[4,96,512]{2,1,0:T(8,128)}, u32[]{:S(2)}) copy-start(f32[4,96,512]{2,1,0:T(8,128)} %get-tuple-element.24) | copy-start | bytes 2359300
  138.3 32.1 %collective-permute-start.10 = (bf16[4,96,512]{2,1,0:T(8,128)(2,1)}, bf16[4,96,512]{2,1,0:T(8,128)(2,1)}, u32[]{:S(2)}, u32[]{:S(2)}) collective-permute-start(bf16[4,96,512]{2,1,0:T(8,128)(2,1)} %get-tuple-element.25), channel_id=1, source_target_pairs={{4,0},{8,4},{12,8},{16,12},{20,16},{24,20},{28,24},{32,28},{36,32}... | collective-permute-start | bytes 1179656 | tf_op jit(solution)/shard_map/ppermute | solution.py:296
  160.1 13.5 %collective-permute-start.11 = (bf16[4,96,512]{2,1,0:T(8,128)(2,1)}, bf16[4,96,512]{2,1,0:T(8,128)(2,1)}, u32[]{:S(2)}, u32[]{:S(2)}) collective-permute-start(bf16[4,96,512]{2,1,0:T(8,128)(2,1)} %get-tuple-element.26), channel_id=1, source_target_pairs={{0,4},{4,8},{8,12},{12,16},{16,20},{20,24},{24,28},{28,32},{32,36}... | collective-permute-start | bytes 1179656 | tf_op jit(solution)/shard_map/ppermute | solution.py:296
  162.0 22.0 %copy-start.11 = (bf16[4,96,512]{2,1,0:T(8,128)(2,1)}, bf16[4,96,512]{2,1,0:T(8,128)(2,1)S(1)}, u32[]{:S(2)}) copy-start(bf16[4,96,512]{2,1,0:T(8,128)(2,1)S(1)} %collective-permute-done.19) | copy-start | bytes 1179652
  162.0 12.5 %collective-permute-start.6 = (bf16[4,96,512]{2,1,0:T(8,128)(2,1)}, bf16[4,96,512]{2,1,0:T(8,128)(2,1)}, u32[]{:S(2)}, u32[]{:S(2)}) collective-permute-start(bf16[4,96,512]{2,1,0:T(8,128)(2,1)} %get-tuple-element.21), channel_id=1, source_target_pairs={{4,0},{8,4},{12,8},{16,12},{20,16},{24,20},{28,24},{32,28},{36,32}... | collective-permute-start | bytes 1179656 | tf_op jit(solution)/shard_map/ppermute | solution.py:296
  168.4 15.6 %copy-start.12 = (bf16[4,96,512]{2,1,0:T(8,128)(2,1)}, bf16[4,96,512]{2,1,0:T(8,128)(2,1)S(1)}, u32[]{:S(2)}) copy-start(bf16[4,96,512]{2,1,0:T(8,128)(2,1)S(1)} %collective-permute-done.14) | copy-start | bytes 1179652
  168.4 13.1 %collective-permute-start.7 = (bf16[4,96,512]{2,1,0:T(8,128)(2,1)}, bf16[4,96,512]{2,1,0:T(8,128)(2,1)}, u32[]{:S(2)}, u32[]{:S(2)}) collective-permute-start(bf16[4,96,512]{2,1,0:T(8,128)(2,1)} %get-tuple-element.22), channel_id=1, source_target_pairs={{0,4},{4,8},{8,12},{12,16},{16,20},{20,24},{24,28},{28,32},{32,36}... | collective-permute-start | bytes 1179656 | tf_op jit(solution)/shard_map/ppermute | solution.py:296
  181.5 36.3 %copy-start.6 = (f32[4,96,512]{2,1,0:T(8,128)S(1)}, f32[4,96,512]{2,1,0:T(8,128)}, u32[]{:S(2)}) copy-start(f32[4,96,512]{2,1,0:T(8,128)} %get-tuple-element.27) | copy-start | bytes 2359300
  181.5 36.3 %copy-start.8 = (f32[4,96,512]{2,1,0:T(8,128)S(1)}, f32[4,96,512]{2,1,0:T(8,128)}, u32[]{:S(2)}) copy-start(f32[4,96,512]{2,1,0:T(8,128)} %get-tuple-element.24) | copy-start | bytes 2359300
  181.5 36.3 %copy-start.9 = (f32[4,96,512]{2,1,0:T(8,128)S(1)}, f32[4,96,512]{2,1,0:T(8,128)}, u32[]{:S(2)}) copy-start(f32[4,96,512]{2,1,0:T(8,128)} %get-tuple-element.20) | copy-start | bytes 2359300
  184.0 8.5 %collective-permute-start.20 = (bf16[4,96,512]{2,1,0:T(8,128)(2,1)S(1)}, bf16[4,96,512]{2,1,0:T(8,128)(2,1)S(1)}, u32[]{:S(2)}, u32[]{:S(2)}) collective-permute-start(bf16[4,96,512]{2,1,0:T(8,128)(2,1)S(1)} %get-tuple-element.47), channel_id=1, source_target_pairs={{0,2},{1,3},{2,0},{3,1},{4,6},{5,7},{6,4},{7,5},{8,10},{9,11},{10,... | collective-permute-start | bytes 1179656 | tf_op jit(solution)/shard_map/ppermute | solution.py:300
  184.3 16.6 %collective-permute-start.8 = (bf16[4,96,512]{2,1,0:T(8,128)(2,1)S(1)}, bf16[4,96,512]{2,1,0:T(8,128)(2,1)S(1)}, u32[]{:S(2)}, u32[]{:S(2)}) collective-permute-start(bf16[4,96,512]{2,1,0:T(8,128)(2,1)S(1)} %get-tuple-element.48), channel_id=1, source_target_pairs={{0,2},{1,3},{2,0},{3,1},{4,6},{5,7},{6,4},{7,5},{8,10},{9,11},{10,... | collective-permute-start | bytes 1179656 | tf_op jit(solution)/shard_map/ppermute | solution.py:300
  187.1 22.3 %collective-permute-start.12 = (bf16[4,96,512]{2,1,0:T(8,128)(2,1)S(1)}, bf16[4,96,512]{2,1,0:T(8,128)(2,1)S(1)}, u32[]{:S(2)}, u32[]{:S(2)}) collective-permute-start(bf16[4,96,512]{2,1,0:T(8,128)(2,1)S(1)} %get-tuple-element.49), channel_id=1, source_target_pairs={{0,2},{1,3},{2,0},{3,1},{4,6},{5,7},{6,4},{7,5},{8,10},{9,11},{10,... | collective-permute-start | bytes 1179656 | tf_op jit(solution)/shard_map/ppermute | solution.py:300
  187.3 30.5 %collective-permute-start.16 = (bf16[4,96,512]{2,1,0:T(8,128)(2,1)S(1)}, bf16[4,96,512]{2,1,0:T(8,128)(2,1)S(1)}, u32[]{:S(2)}, u32[]{:S(2)}) collective-permute-start(bf16[4,96,512]{2,1,0:T(8,128)(2,1)S(1)} %get-tuple-element.50), channel_id=1, source_target_pairs={{0,2},{1,3},{2,0},{3,1},{4,6},{5,7},{6,4},{7,5},{8,10},{9,11},{10,... | collective-permute-start | bytes 1179656 | tf_op jit(solution)/shard_map/ppermute | solution.py:300
  220.4 13.6 %copy-start.1 = (f32[4,96,512]{2,1,0:T(8,128)}, f32[4,96,512]{2,1,0:T(8,128)S(1)}, u32[]{:S(2)}) copy-start(f32[4,96,512]{2,1,0:T(8,128)S(1)} %get-tuple-element.46.refs_0_) | copy-start | bytes 2359300
  220.4 6.6 %collective-permute-start.21 = (f32[4,96,512]{2,1,0:T(8,128)S(1)}, f32[4,96,512]{2,1,0:T(8,128)S(1)}, u32[]{:S(2)}, u32[]{:S(2)}) collective-permute-start(f32[4,96,512]{2,1,0:T(8,128)S(1)} %get-tuple-element.43.refs_0_), channel_id=1, source_target_pairs={{0,1},{1,0},{2,3},{3,2},{4,5},{5,4},{6,7},{7,6},{8,9},{9,8},{10,11... | collective-permute-start | bytes 2359304 | tf_op jit(solution)/shard_map/ppermute | solution.py:300
  225.1 8.9 %collective-permute-start.17 = (f32[4,96,512]{2,1,0:T(8,128)S(1)}, f32[4,96,512]{2,1,0:T(8,128)}, u32[]{:S(2)}, u32[]{:S(2)}) collective-permute-start(f32[4,96,512]{2,1,0:T(8,128)S(1)} %get-tuple-element.45.refs_0_), channel_id=1, source_target_pairs={{0,1},{1,0},{2,3},{3,2},{4,5},{5,4},{6,7},{7,6},{8,9},{9,8},{10,11... | collective-permute-start | bytes 2359304 | tf_op jit(solution)/shard_map/ppermute | solution.py:300
  225.1 16.0 %collective-permute-start.13 = (f32[4,96,512]{2,1,0:T(8,128)S(1)}, f32[4,96,512]{2,1,0:T(8,128)}, u32[]{:S(2)}, u32[]{:S(2)}) collective-permute-start(f32[4,96,512]{2,1,0:T(8,128)S(1)} %get-tuple-element.44.refs_0_), channel_id=1, source_target_pairs={{0,1},{1,0},{2,3},{3,2},{4,5},{5,4},{6,7},{7,6},{8,9},{9,8},{10,11... | collective-permute-start | bytes 2359304 | tf_op jit(solution)/shard_map/ppermute | solution.py:300
  225.6 22.8 %collective-permute-start.9 = (f32[4,96,512]{2,1,0:T(8,128)S(1)}, f32[4,96,512]{2,1,0:T(8,128)S(1)}, u32[]{:S(2)}, u32[]{:S(2)}) collective-permute-start(f32[4,96,512]{2,1,0:T(8,128)S(1)} %get-tuple-element.46.refs_0_), channel_id=1, source_target_pairs={{0,1},{1,0},{2,3},{3,2},{4,5},{5,4},{6,7},{7,6},{8,9},{9,8},{10,11... | collective-permute-start | bytes 2359304 | tf_op jit(solution)/shard_map/ppermute | solution.py:300
  (6 other events, 35.7 us)

commit v2 on v0

v2 whole, which is shorter than its diff:
```python
import functools
import math

import jax
import jax.numpy as jnp
import numpy as np
from jax import lax
from jax.experimental import pallas as pl
from jax.experimental.pallas import tpu as pltpu
from jax.sharding import PartitionSpec as P

SEG = 1024
HALF = 96
LANES = 128
GROUPS = SEG // LANES
PAIR = 2 * LANES
CHUNKS = ((0, 3), (3, 3), (6, 2))
FOLD = 32
TILE = 32
SUB = 16
PITCH = 104
SOURCES = 4
SLOT = 16
COLS = 256


def small_tables():
    k = GROUPS * np.arange(LANES)[None, :] + np.arange(GROUPS)[:, None]
    step = np.arange(FOLD)

    def waves(stride):
        phase = (stride * step[None, :, None] * k[:, None, :]) % (2 * SEG)
        angle = phase * (2.0 * math.pi / (2 * SEG))
        return np.stack([np.cos(angle), np.sin(angle)], axis=1).astype(np.float32)

    return waves(FOLD), waves(1)


def table_kernel(coarse_ref, fine_ref, hi_ref, lo_ref):
    fine_cos = fine_ref[0, 0]
    fine_sin = fine_ref[0, 1]

    def row_block(a, carry):
        base_cos = jnp.concatenate([coarse_ref[0, 0, pl.ds(a, 8, stride=0), :]] * (FOLD // 8), axis=0)
        base_sin = jnp.concatenate([coarse_ref[0, 1, pl.ds(a, 8, stride=0), :]] * (FOLD // 8), axis=0)
        real = base_cos * fine_cos - base_sin * fine_sin
        imag = -(base_sin * fine_cos + base_cos * fine_sin)
        rows = pl.ds(pl.multiple_of(a * FOLD, FOLD), FOLD)
        for part, lane in ((real, 0), (imag, LANES)):
            top = part.astype(jnp.bfloat16)
            hi_ref[0, rows, lane:lane + LANES] = top
            lo_ref[0, rows, lane:lane + LANES] = (part - top.astype(jnp.float32)).astype(jnp.bfloat16)
        return carry

    lax.fori_loop(0, FOLD, row_block, 0)


def make_tables(first, count, coarse, fine):
    shape = jax.ShapeDtypeStruct((count, SEG, PAIR), jnp.bfloat16)
    small = pl.BlockSpec((1, 2, FOLD, LANES), lambda p: (first + p, 0, 0, 0))
    large = pl.BlockSpec((1, SEG, PAIR), lambda p: (p, 0, 0))
    return pl.pallas_call(
        table_kernel,
        grid=(count,),
        in_specs=[small, small],
        out_specs=[large, large],
        out_shape=[shape, shape],
        name="tables",
    )(coarse, fine)


def normalize_kernel(half_ref, samples_ref, scale_ref, out_ref, buffer_ref, sems, *, seg_count, windows):
    step = pl.program_id(0)
    steps = pl.num_programs(0)
    per_channel = samples_ref.shape[1]
    pieces = SEG // LANES
    pairs = pieces // 2
    blocks = seg_count * pairs
    slot = step % 2

    def copy(at, into):
        first = half_ref[0] * HALF + at * TILE
        return pltpu.make_async_copy(
            samples_ref.at[pl.ds(first, TILE)],
            buffer_ref.at[into, :, pl.ds(0, per_channel), :],
            sems.at[into],
        )

    @pl.when(step == 0)
    def _():
        copy(0, 0).start()

    @pl.when(step + 1 < steps)
    def _():
        copy(step + 1, 1 - slot).start()

    copy(step, slot).wait()
    flat = buffer_ref.reshape(2 * TILE * PITCH, LANES)
    base = slot * (TILE * PITCH)

    def rows(w, n, piece):
        start = base + (n * pieces + piece) * windows + w
        return flat[pl.ds(start, TILE, stride=PITCH), :].astype(jnp.float32)

    scale = scale_ref[...]
    live = scale[:, windows * blocks:windows * blocks + 1]
    for w in range(windows):
        total = jnp.zeros((TILE, LANES), jnp.float32)
        for n in range(seg_count):
            for pair in range(pairs):
                column = w * blocks + n * pairs + pair
                one = rows(w, n, 2 * pair)
                two = rows(w, n, 2 * pair + 1)
                weight = scale[:, column:column + 1]
                total = total + (one * one + two * two) * (weight * weight)
        energy = jnp.sum(total, axis=1, keepdims=True) * (1.0 / (seg_count * SEG))
        factor = live * lax.rsqrt(energy + 1e-06)
        for n in range(seg_count):
            for pair in range(pairs):
                column = w * blocks + n * pairs + pair
                weight = scale[:, column:column + 1] * factor
                for piece in (2 * pair, 2 * pair + 1):
                    value = rows(w, n, piece) * weight
                    out_ref[w * seg_count + n, :, piece * LANES:(piece + 1) * LANES] = value.astype(jnp.bfloat16)


def normalize_half(half, samples_rows, scales, seg_count, windows):
    steps = HALF // TILE
    return pl.pallas_call(
        functools.partial(normalize_kernel, seg_count=seg_count, windows=windows),
        grid_spec=pltpu.PrefetchScalarGridSpec(
            num_scalar_prefetch=1,
            grid=(steps,),
            in_specs=[
                pl.BlockSpec(memory_space=pl.ANY),
                pl.BlockSpec((TILE, scales.shape[1]), lambda i, h: (h[0] * steps + i, 0)),
            ],
            out_specs=pl.BlockSpec((windows * seg_count, TILE, SEG), lambda i, h: (0, i, 0)),
            scratch_shapes=[
                pltpu.VMEM((2, TILE, PITCH, LANES), jnp.int32),
                pltpu.SemaphoreType.DMA((2,)),
            ],
        ),
        out_shape=jax.ShapeDtypeStruct((windows * seg_count, HALF, SEG), jnp.bfloat16),
        name="normalize",
    )(half, samples_rows, scales)


def source_kernel(offsets_ref, samples_ref, scale_ref, out_ref, sorted_ref, buffer_ref, rows_ref, sems, *,
                  seg_count, windows):
    pieces = SEG // LANES
    pairs = pieces // 2
    blocks = seg_count * pairs
    channels = scale_ref.shape[0]
    per_channel = samples_ref.shape[1]
    given = [offsets_ref[j] for j in range(SOURCES)]
    ranks = []
    for j in range(SOURCES):
        rank = jnp.int32(0)
        for i in range(SOURCES):
            if i != j:
                ahead = given[i] <= given[j] if i < j else given[i] < given[j]
                rank = rank + jnp.where(ahead, 1, 0)
        ranks.append(rank)
    order = []
    for r in range(SOURCES):
        offset = jnp.int32(0)
        origin = jnp.int32(0)
        for j in range(SOURCES):
            hit = ranks[j] == r
            offset = jnp.where(hit, given[j], offset)
            origin = jnp.where(hit, j, origin)
        sorted_ref[r] = offset
        sorted_ref[SOURCES + r] = origin
        order.append(offset)
    copies = []
    for r in range(SOURCES):
        copy = pltpu.make_async_copy(
            samples_ref.at[order[r]], buffer_ref.at[r, pl.ds(0, per_channel), :], sems.at[r]
        )
        copy.start()
        copies.append(copy)
    channel = lax.broadcasted_iota(jnp.int32, scale_ref.shape, 0)
    lane = lax.broadcasted_iota(jnp.int32, (8, scale_ref.shape[1]), 1)
    segment = lax.broadcasted_iota(jnp.int32, (8, scale_ref.shape[1]), 0)
    valid = lax.broadcasted_iota(jnp.int32, (8, LANES), 0) < seg_count
    rows_ref[...] = jnp.zeros(rows_ref.shape, jnp.float32)
    for r in range(SOURCES):
        picked = jnp.sum(jnp.where(channel == order[r], scale_ref[...], 0.0), axis=0, keepdims=True)
        picked = jnp.broadcast_to(picked, (8, scale_ref.shape[1]))
        live = jnp.sum(jnp.where(lane == windows * blocks, picked, 0.0), axis=1, keepdims=True)
        copies[r].wait()
        for w in range(windows):
            parts = []
            total = jnp.zeros((8, LANES), jnp.float32)
            for pair in range(pairs):
                column = w * blocks + segment * pairs + pair
                weight = jnp.sum(jnp.where(lane == column, picked, 0.0), axis=1, keepdims=True)
                for piece in (2 * pair, 2 * pair + 1):
                    raw = buffer_ref[r, pl.ds(piece * windows + w, 8, stride=pieces * windows), :]
                    part = jnp.where(valid, raw.astype(jnp.float32), 0.0) * weight
                    total = total + part * part
                    parts.append(part)
            energy = jnp.sum(jnp.sum(total, axis=1, keepdims=True), axis=0, keepdims=True)
            factor = live * lax.rsqrt(energy * (1.0 / (seg_count * SEG)) + 1e-06)
            for piece in range(pieces):
                rows_ref[r, pl.ds(w * seg_count, seg_count), piece * LANES:(piece + 1) * LANES] = (
                    parts[piece] * factor
                )[:seg_count]
        rows_ref[r, pl.ds(windows * seg_count, 1), :] = jnp.full((1, SEG), 1, jnp.float32) * (
            order[r] + 1
        ).astype(jnp.float32)
        out_ref[r] = rows_ref[r].astype(jnp.bfloat16)


def source_rows(offsets, samples_rows, scales, seg_count, windows):
    return pl.pallas_call(
        functools.partial(source_kernel, seg_count=seg_count, windows=windows),
        grid_spec=pltpu.PrefetchScalarGridSpec(
            num_scalar_prefetch=1,
            grid=(1,),
            in_specs=[
                pl.BlockSpec(memory_space=pl.ANY),
                pl.BlockSpec(scales.shape, lambda i, h: (0, 0)),
            ],
            out_specs=[
                pl.BlockSpec((SOURCES, SLOT, SEG), lambda i, h: (0, 0, 0)),
                pl.BlockSpec(memory_space=pltpu.SMEM),
            ],
            scratch_shapes=[
                pltpu.VMEM((SOURCES, 128, LANES), jnp.int32),
                pltpu.VMEM((SOURCES, SLOT, SEG), jnp.float32),
                pltpu.SemaphoreType.DMA((SOURCES,)),
            ],
        ),
        out_shape=[
            jax.ShapeDtypeStruct((SOURCES, SLOT, SEG), jnp.bfloat16),
            jax.ShapeDtypeStruct((2 * SOURCES,), jnp.int32),
        ],
        name="sources",
    )(offsets, samples_rows, scales)


def cross_kernel(limits_ref, near_ref, far_ref, own_src_ref, above_src_ref, below_src_ref, table_ref,
                 own_ref, up_ref, down_ref, band_ref, src_ref, plus_ref, minus_ref):
    step = pl.program_id(0)
    count = near_ref.shape[0]
    groups = table_ref.shape[0]
    src_rows = 2 * SLOT

    @pl.when(step == 0)
    def _():
        for which, ref in enumerate((own_src_ref, above_src_ref, below_src_ref)):
            rows = ref[...].reshape(SOURCES * src_rows, SEG)
            at = pl.ds(which * SOURCES * src_rows, SOURCES * src_rows)
            for g in range(groups):
                spec = jnp.dot(rows, table_ref[g], preferred_element_type=jnp.float32)
                spec = spec.astype(jnp.bfloat16).astype(jnp.float32)
                real = spec[:, :LANES]
                imag = spec[:, LANES:]
                src_ref[g, at, :] = real
                plus_ref[g, at, :] = real + imag
                minus_ref[g, at, :] = imag - real

    for part, ref in ((0, near_ref), (1, far_ref)):
        rows = ref[...].reshape(count * TILE, SEG)
        at = pl.ds(part * count * TILE, count * TILE)
        for g in range(groups):
            spec = jnp.dot(rows, table_ref[g], preferred_element_type=jnp.float32)
            spec = spec.astype(jnp.bfloat16).astype(jnp.float32)
            band_ref[2 * g, at, :] = spec[:, :LANES]
            band_ref[2 * g + 1, at, :] = spec[:, LANES:]

    def products(which, members, out_ref, g, row):
        lane = pl.multiple_of(g * PAIR, PAIR)
        real_lanes = pl.ds(lane, LANES)
        imag_lanes = pl.ds(pl.multiple_of(lane + LANES, LANES), LANES)
        zero = jnp.zeros((8, LANES), jnp.float32)
        acc = {(t, j): [zero, zero, zero] for t in range(SUB // 8) for j in members}
        for q in range(2 * count):
            band = []
            for t in range(SUB // 8):
                at = pl.ds(q * TILE + row + 8 * t, 8)
                g_re = band_ref[2 * g, at, :]
                g_im = band_ref[2 * g + 1, at, :]
                band.append((g_re, g_im, g_re + g_im))
            spot = q if q < count else SLOT + q - count
            for j in members:
                at = pl.ds((which * SOURCES + j) * src_rows + spot, 8, stride=0)
                s_re = src_ref[g, at, :]
                s_plus = plus_ref[g, at, :]
                s_minus = minus_ref[g, at, :]
                for t in range(SUB // 8):
                    g_re, g_im, g_sum = band[t]
                    a = acc[t, j]
                    a[0] = a[0] + s_re * g_sum
                    a[1] = a[1] + s_minus * g_im
                    a[2] = a[2] + s_plus * g_re
        for j in members:
            real = jnp.concatenate([acc[t, j][0] + acc[t, j][1] for t in range(SUB // 8)], axis=0)
            imag = jnp.concatenate([acc[t, j][0] - acc[t, j][2] for t in range(SUB // 8)], axis=0)
            out_ref[j, pl.ds(row, SUB), real_lanes] = real.astype(out_ref.dtype)
            out_ref[j, pl.ds(row, SUB), imag_lanes] = imag.astype(out_ref.dtype)

    def tile(index, carry):
        g = index // (TILE // SUB)
        row = pl.multiple_of((index % (TILE // SUB)) * SUB, SUB)
        channel = limits_ref[0] + step * TILE + row
        for first in (0, 2):
            pair = (first, first + 1)

            @pl.when(channel + SUB > limits_ref[1 + first])
            def _():
                products(1, pair, up_ref, g, row)

            @pl.when(channel < limits_ref[1 + SOURCES + first + 1])
            def _():
                products(2, pair, down_ref, g, row)

        products(0, (0, 1, 2, 3), own_ref, g, row)
        return carry

    lax.fori_loop(0, groups * (TILE // SUB), tile, 0)


def cross_chunk(limits, near, far, own_src, above_src, below_src, table):
    count = near.shape[0]
    groups = table.shape[0]
    width = groups * PAIR
    src_rows = 3 * SOURCES * 2 * SLOT
    block = pl.BlockSpec((count, TILE, SEG), lambda i, h: (0, i, 0))
    src = pl.BlockSpec((SOURCES, 2 * SLOT, SEG), lambda i, h: (0, 0, 0))
    result = pl.BlockSpec((SOURCES, TILE, width), lambda i, h: (0, i, 0))
    return pl.pallas_call(
        cross_kernel,
        grid_spec=pltpu.PrefetchScalarGridSpec(
            num_scalar_prefetch=1,
            grid=(HALF // TILE,),
            in_specs=[block, block, src, src, src, pl.BlockSpec((groups, SEG, PAIR), lambda i, h: (0, 0, 0))],
            out_specs=[result, result, result],
            scratch_shapes=[
                pltpu.VMEM((2 * groups, 2 * count * TILE, LANES), jnp.float32),
                pltpu.VMEM((groups, src_rows, LANES), jnp.float32),
                pltpu.VMEM((groups, src_rows, LANES), jnp.float32),
                pltpu.VMEM((groups, src_rows, LANES), jnp.float32),
            ],
        ),
        out_shape=[
            jax.ShapeDtypeStruct((SOURCES, HALF, width), jnp.float32),
            jax.ShapeDtypeStruct((SOURCES, HALF, width), jnp.bfloat16),
            jax.ShapeDtypeStruct((SOURCES, HALF, width), jnp.bfloat16),
        ],
        name="cross",
    )(limits, near, far, own_src, above_src, below_src, table)


def select_kernel(sorted_ref, place_ref, own_ref, below_ref, above_ref, kept_ref, passed_ref):
    base = place_ref[0]
    lower = place_ref[1] == 0
    index = base + lax.broadcasted_iota(jnp.int32, (HALF, LANES), 0)
    for j in range(SOURCES):
        below_source = index < sorted_ref[j]
        first = jnp.where(below_source, 1, 0)
        keep = first == jnp.where(lower, 1, 0)
        for lane in range(0, own_ref.shape[2], LANES):
            at = (j, slice(None), slice(lane, lane + LANES))
            own = own_ref[at]
            other = jnp.where(below_source, above_ref[at].astype(jnp.float32), below_ref[at].astype(jnp.float32))
            kept_ref[at] = jnp.where(keep, own, other)
            passed_ref[at] = jnp.where(keep, other, own).astype(jnp.bfloat16)


def select_rows(ordered, place, own, from_below, from_above):
    whole = pl.BlockSpec(memory_space=pltpu.VMEM)
    return pl.pallas_call(
        select_kernel,
        in_specs=[pl.BlockSpec(memory_space=pltpu.SMEM), pl.BlockSpec(memory_space=pltpu.SMEM), whole, whole, whole],
        out_specs=[whole, whole],
        out_shape=[jax.ShapeDtypeStruct(own.shape, jnp.float32), jax.ShapeDtypeStruct(own.shape, jnp.bfloat16)],
        name="select",
    )(ordered, place, own, from_below, from_above)


def turned(ordered_ref, mine_ref, mate_ref, top_ref, halve):
    source_row = lax.broadcasted_iota(jnp.int32, (HALF, 2 * HALF), 1)
    target_row = lax.broadcasted_iota(jnp.int32, (HALF, 2 * HALF), 0)
    for j in range(SOURCES):
        wanted = target_row + ordered_ref[j]
        wanted = jnp.where(wanted >= 2 * HALF, wanted - 2 * HALF, wanted)
        turn = jnp.where(source_row == wanted, 1.0, 0.0).astype(jnp.bfloat16)
        rows = jnp.concatenate([mine_ref[j], mate_ref[j]], axis=0)
        top_ref[pl.ds(j * HALF, HALF), :] = jnp.dot(turn, rows, preferred_element_type=jnp.float32).astype(
            jnp.bfloat16
        )
    if halve:
        lane = lax.broadcasted_iota(jnp.int32, (SOURCES * HALF, LANES), 1)
        first = top_ref[:, :LANES].astype(jnp.float32)
        top_ref[:, :LANES] = jnp.where(lane == 0, 0.5 * first, first).astype(jnp.bfloat16)


def folded(top_ref, hi_ref, lo_ref, first, sums):
    for g in range(hi_ref.shape[0]):
        rows = top_ref[:, g * PAIR:(g + 1) * PAIR]
        for table in (hi_ref[g], lo_ref[g]):
            part = lax.dot_general(rows, table, (((1,), (1,)), ((), ())), preferred_element_type=jnp.float32)
            parity = (first + g) % 2
            sums[parity] = part if sums[parity] is None else sums[parity] + part


def early_kernel(ordered_ref, *refs, firsts):
    count = len(firsts)
    tops = refs[4 * count + 2:]
    even_ref, odd_ref = refs[4 * count:4 * count + 2]
    for c, first in enumerate(firsts):
        @pl.when(pl.program_id(0) == 0)
        def _():
            turned(ordered_ref, refs[4 * c], refs[4 * c + 1], tops[c], first == 0)
    sums = [None, None]
    for c, first in enumerate(firsts):
        folded(tops[c], refs[4 * c + 2], refs[4 * c + 3], first, sums)
    even_ref[...] = sums[0]
    odd_ref[...] = sums[1]


def chunk_specs(groups):
    rows = pl.BlockSpec((SOURCES, HALF, groups * PAIR), lambda m, h: (0, 0, 0))
    table = pl.BlockSpec((groups, COLS, PAIR), lambda m, h: (0, m, 0))
    return [rows, rows, table, table]


def early_inverse(ordered, parts, firsts):
    specs, operands, tops = [], [], []
    for part in parts:
        groups = part[2].shape[0]
        specs += chunk_specs(groups)
        operands += list(part)
        tops.append(pltpu.VMEM((SOURCES * HALF, groups * PAIR), jnp.bfloat16))
    block = pl.BlockSpec((SOURCES * HALF, COLS), lambda m, h: (0, m))
    shape = jax.ShapeDtypeStruct((SOURCES * HALF, SEG), jnp.float32)
    return pl.pallas_call(
        functools.partial(early_kernel, firsts=firsts),
        grid_spec=pltpu.PrefetchScalarGridSpec(
            num_scalar_prefetch=1,
            grid=(SEG // COLS,),
            in_specs=specs,
            out_specs=[block, block],
            scratch_shapes=tops,
        ),
        out_shape=[shape, shape],
        name="early",
    )(ordered, *operands)


def last_kernel(ordered_ref, mine_ref, mate_ref, hi_ref, lo_ref, even_ref, odd_ref, out_ref, top_ref, stage_ref, sem,
                *, first, scale):
    m = pl.program_id(0)

    @pl.when(m == 0)
    def _():
        turned(ordered_ref, mine_ref, mate_ref, top_ref, first == 0)

    sums = [even_ref[...], odd_ref[...]]
    folded(top_ref, hi_ref, lo_ref, first, sums)
    stage_ref[m, 0] = (sums[0] - sums[1]) * scale
    stage_ref[m, 1] = (sums[0] + sums[1]) * scale

    def copy(step, side, j):
        lane = pl.multiple_of(side * SEG + step * COLS, COLS)
        return pltpu.make_async_copy(
            stage_ref.at[step, side, pl.ds(j * HALF, HALF), :],
            out_ref.at[ordered_ref[SOURCES + j], :, pl.ds(lane, COLS)],
            sem.at[step, side, j],
        )

    for side in range(2):
        for j in range(SOURCES):
            copy(m, side, j).start()

    @pl.when(m == pl.num_programs(0) - 1)
    def _():
        for step in range(SEG // COLS):
            for side in range(2):
                for j in range(SOURCES):
                    copy(step, side, j).wait()


def last_inverse(ordered, part, even, odd, first, scale):
    groups = part[2].shape[0]
    block = pl.BlockSpec((SOURCES * HALF, COLS), lambda m, h: (0, m))
    return pl.pallas_call(
        functools.partial(last_kernel, first=first, scale=scale),
        grid_spec=pltpu.PrefetchScalarGridSpec(
            num_scalar_prefetch=1,
            grid=(SEG // COLS,),
            in_specs=chunk_specs(groups) + [block, block],
            out_specs=pl.BlockSpec(memory_space=pl.ANY),
            scratch_shapes=[
                pltpu.VMEM((SOURCES * HALF, groups * PAIR), jnp.bfloat16),
                pltpu.VMEM((SEG // COLS, 2, SOURCES * HALF, COLS), jnp.float32),
                pltpu.SemaphoreType.DMA((SEG // COLS, 2, SOURCES)),
            ],
        ),
        out_shape=jax.ShapeDtypeStruct((SOURCES, HALF, 2 * SEG), jnp.float32),
        name="last",
    )(ordered, *part, even, odd)


def block_scale(exponents):
    levels = jnp.arange(5, dtype=jnp.int32)
    powers = jnp.exp2(levels.astype(jnp.float32))
    return jnp.sum(jnp.where(exponents[..., None] == levels, powers, 0.0), axis=-1)


def passed_along(block, axis, distance):
    devices = range(lax.axis_size(axis))
    route = [(i - distance, i) for i in devices if i - distance in devices]
    return lax.ppermute(block, axis, route)


def partner(block, bit):
    return lax.ppermute(block, "win", [(i, i ^ bit) for i in range(lax.axis_size("win"))])


def after(value, *others):
    return lax.optimization_barrier((value,) + others)[0]


def shards(samples, exponents, alive, offsets):
    channels, windows, length = samples.shape
    seg_count = length // SEG
    place = lax.axis_index("win")
    core = place & 1
    upper_half = place >> 1

    samples_rows = samples.reshape(channels, windows, length // LANES, LANES)
    samples_rows = samples_rows.transpose(0, 2, 1, 3).reshape(channels, windows * (length // LANES), LANES)
    scales = block_scale(exponents).reshape(channels, -1)
    scales = jnp.concatenate([scales, alive.astype(jnp.float32).reshape(channels, 1)], axis=1)

    own_src, ordered = source_rows(offsets, samples_rows, scales, seg_count, windows)
    own_src = jnp.concatenate([own_src, partner(own_src, 1)], axis=1)
    above_src = passed_along(own_src, "chan", -1)
    below_src = passed_along(own_src, "chan", 1)

    sent = normalize_half((1 - core).reshape(1), samples_rows, scales, seg_count, windows)
    far = partner(sent, 1)
    near = normalize_half(core.reshape(1), samples_rows, scales, seg_count, windows)
    coarse, fine = (jnp.asarray(t) for t in small_tables())

    flag = windows * seg_count
    above_off = above_src[:, flag, 0].astype(jnp.int32)
    below_off = below_src[:, flag, 0].astype(jnp.int32)
    limits = jnp.concatenate(
        [(core * HALF).reshape(1), jnp.where(above_off == 0, channels, above_off - 1), below_off - 1]
    ).astype(jnp.int32)
    where_am_i = jnp.stack([core * HALF, upper_half]).astype(jnp.int32)
    scale = 2.0 / float(2 * SEG * windows * lax.axis_size("win") * seg_count * SEG)

    tables = [make_tables(first, count, coarse, fine) for first, count in CHUNKS]
    total_chunks = len(CHUNKS)
    crossed, returned, selected, parts = [], [], [], []

    def finish(c):
        kept, moved = selected[c]
        total = (kept + moved.astype(jnp.float32)).astype(jnp.bfloat16)
        parts.append((total, partner(total, 1)) + tuple(tables[c]))

    for c in range(total_chunks):
        gate = limits
        if c >= 2:
            gate = after(limits, selected[c - 2][0])
        own, to_above, to_below = cross_chunk(gate, near, far, own_src, above_src, below_src, tables[c][0])
        crossed.append(own)
        returned.append((passed_along(to_above, "chan", 1), passed_along(to_below, "chan", -1)))
        if c >= 1:
            kept, moved = select_rows(after(ordered, own), where_am_i, crossed[c - 1], *returned[c - 1])
            selected.append((kept, partner(moved, 2)))
    c = total_chunks - 1
    kept, moved = select_rows(ordered, where_am_i, crossed[c], *returned[c])
    selected.append((kept, partner(moved, 2)))
    for c in range(total_chunks):
        finish(c)
    firsts = tuple(first for first, _ in CHUNKS)
    even, odd = early_inverse(ordered, parts[:-1], firsts[:-1])
    return last_inverse(ordered, parts[-1], even, odd, firsts[-1], scale)


def solution(mesh):
    placed = (P("chan", "win", None), P("chan", "win", None), P("chan"), P("chan"))
    return jax.shard_map(
        shards, mesh=mesh, in_specs=placed, out_specs=P("chan", "win", None), check_vma=False
    )
```

time: 639 us -> 200 us (0.31)
  the two profiles are of different devices: /device:TPU:37 before, /device:TPU:69 now
where the time goes in v2:
time: 200 us; the launch traced here: 199 us
  Pallas kernels  118 us (59%)
  starting transfers between devices  39.3 us (20%)
  waiting for transfers between devices  29 us (14%)
  local copies, waits for them, and re-layouts  8.55 us (4%)
  other arithmetic  4.24 us (2%)
    pallas_call x3, Pallas kernels, cross_chunk(): pl.pallas_call(cross_kernel, grid_spec=pltpu.PrefetchScalarGridSpec(num_s...  53.8 us
    ppermute x8, starting transfers between devices, passed_along(): return lax.ppermute(block, axis, route)  33.4 us
    pallas_call x2, Pallas kernels, normalize_half(): pl.pallas_call(functools.partial(normalize_kernel, seg_count=seg_count, w...  25.9 us
    ppermute x8, waiting for transfers between devices, partner(): lax.ppermute(block, 'win', [(i, i ^ bit) for i in range(lax.axis_size('wi...  17.7 us
    ppermute x8, waiting for transfers between devices, passed_along(): return lax.ppermute(block, axis, route)  11.3 us
    pallas_call x3, Pallas kernels, make_tables(): pl.pallas_call(table_kernel, grid=(count,), in_specs=[small, small], out_...  10.1 us
    pallas_call x3, Pallas kernels, select_rows(): pl.pallas_call(select_kernel, in_specs=[pl.BlockSpec(memory_space=pltpu.S...  8.82 us
    pallas_call x1, Pallas kernels, early_inverse(): pl.pallas_call(functools.partial(early_kernel, firsts=firsts), grid_spec=...  8.48 us
  transfers between devices with their start and end apart: 16, of which 4 were waited for; matrix products, arithmetic and copies ran while one was open for 1% of the time, Pallas kernels for 38%

profile of v2, /device:TPU:69, one launch (start us, length us, event | category | flops | bytes accessed | tf_op | source)
XLA Modules:
  0.0 199.3 jit_solution(5010794276450053934)
XLA Ops:
  0.0 0.9 select_reduce_fusion
  2.6 13.0 %normalize.3 = bf16[12,96,1024]{2,1,0:T(8,128)(2,1)} custom-call(s32[1]{0:T(128)} %bitcast.10.half_ref, s32[192,96,128]{2,1,0:T(8,128)} %bitcast.11, f32[192,49]{1,0:T(8,128)} %pad_maximum_fusion.scale_ref), custom_call_target="tpu_custom_call" | custom-call | tf_op jit(solution)/shard_map/normalize/pallas_call | solution.py:129
  16.3 3.8 %sources.1 = (bf16[4,16,1024]{2,1,0:T(8,128)(2,1)}, s32[8]{0:T(128)}) custom-call(s32[4]{0:T(128)} %offsets_ref.1, s32[192,96,128]{2,1,0:T(8,128)} %bitcast.12, f32[192,49]{1,0:T(8,128)} %pad_maximum_fusion.scale_ref), custom_call_target="tpu_custom_call" | custom-call | tf_op jit(solution)/shard_map/sources/pallas_call | solution.py:217
  20.3 0.9 constant_dynamic-update-slice_fusion.1
  21.8 3.2 %collective-permute-start.2 = (bf16[4,32,1024]{2,1,0:T(8,128)(2,1)S(1)}, bf16[4,32,1024]{2,1,0:T(8,128)(2,1)S(1)}, u32[]{:S(2)}, u32[]{:S(2)}) collective-permute-start(bf16[4,32,1024]{2,1,0:T(8,128)(2,1)S(1)} %constant_dynamic-update-slice_fusion.own_src_ref), channel_id=1, source_target_pairs={{0,4},{4,8},{8,12},{12,16},{16,20},{20,24},{24,28},{28,32},{32,36}... | collective-permute-start | bytes 786440 | tf_op jit(solution)/shard_map/ppermute | solution.py:517
  25.1 5.1 %collective-permute-start.1 = (bf16[4,32,1024]{2,1,0:T(8,128)(2,1)S(1)}, bf16[4,32,1024]{2,1,0:T(8,128)(2,1)S(1)}, u32[]{:S(2)}, u32[]{:S(2)}) collective-permute-start(bf16[4,32,1024]{2,1,0:T(8,128)(2,1)S(1)} %constant_dynamic-update-slice_fusion.own_src_ref), channel_id=1, source_target_pairs={{4,0},{8,4},{12,8},{16,12},{20,16},{24,20},{28,24},{32,28},{36,32}... | collective-permute-start | bytes 786440 | tf_op jit(solution)/shard_map/ppermute | solution.py:517
  30.2 12.9 %normalize.2.near_ref = bf16[12,96,1024]{2,1,0:T(8,128)(2,1)} custom-call(s32[1]{0:T(128)} %bitcast.7.half_ref, s32[192,96,128]{2,1,0:T(8,128)} %bitcast.13, f32[192,49]{1,0:T(8,128)} %pad_maximum_fusion.scale_ref), custom_call_target="tpu_custom_call" | custom-call | tf_op jit(solution)/shard_map/normalize/pallas_call | solution.py:129
  43.1 3.7 %tables.4 = (bf16[3,1024,256]{2,1,0:T(8,128)(2,1)}, bf16[3,1024,256]{2,1,0:T(8,128)(2,1)}) custom-call(f32[8,2,32,128]{3,2,1,0:T(8,128)} %constant.24.clone.coarse_ref, f32[8,2,32,128]{3,2,1,0:T(8,128)} %constant.25.clone.fine_ref), custom_call_target="tpu_custom_call" | custom-call | tf_op jit(solution)/shard_map/tables/pallas_call | solution.py:62
  47.8 1.4 copy-done
  49.2 19.7 %cross.4 = (f32[4,96,768]{2,1,0:T(8,128)}, bf16[4,96,768]{2,1,0:T(8,128)(2,1)}, bf16[4,96,768]{2,1,0:T(8,128)(2,1)}) custom-call(s32[9]{0:T(128)} %pad_add_fusion.1.limits_ref, bf16[12,96,1024]{2,1,0:T(8,128)(2,1)} %normalize.2.near_ref, bf16[12,96,1024]{2,1,0:T(8,128)(2,1)} %copy-done, bf16[4,32,1024]{2,1,0:T(8,128)(2,1)} %copy-done.1, ...), custom_call_target="tpu_custom_call" | custom-call | tf_op jit(solution)/shard_map/cross/pallas_call | solution.py:334
  68.9 1.9 collective-permute-start.4
  70.8 6.4 %collective-permute-start.5 = (bf16[4,96,768]{2,1,0:T(8,128)(2,1)}, bf16[4,96,768]{2,1,0:T(8,128)(2,1)S(1)}, u32[]{:S(2)}, u32[]{:S(2)}) collective-permute-start(bf16[4,96,768]{2,1,0:T(8,128)(2,1)} %get-tuple-element.41), channel_id=1, source_target_pairs={{4,0},{8,4},{12,8},{16,12},{20,16},{24,20},{28,24},{32,28},{36,32}... | collective-permute-start | bytes 1769480 | tf_op jit(solution)/shard_map/ppermute | solution.py:517
  77.2 3.7 %tables.3 = (bf16[3,1024,256]{2,1,0:T(8,128)(2,1)}, bf16[3,1024,256]{2,1,0:T(8,128)(2,1)}) custom-call(f32[8,2,32,128]{3,2,1,0:T(8,128)} %constant.24.clone.coarse_ref, f32[8,2,32,128]{3,2,1,0:T(8,128)} %constant.25.clone.fine_ref), custom_call_target="tpu_custom_call" | custom-call | tf_op jit(solution)/shard_map/tables/pallas_call | solution.py:62
  80.9 19.7 %cross.3 = (f32[4,96,768]{2,1,0:T(8,128)}, bf16[4,96,768]{2,1,0:T(8,128)(2,1)}, bf16[4,96,768]{2,1,0:T(8,128)(2,1)}) custom-call(s32[9]{0:T(128)} %pad_add_fusion.1.limits_ref, bf16[12,96,1024]{2,1,0:T(8,128)(2,1)} %normalize.2.near_ref, bf16[12,96,1024]{2,1,0:T(8,128)(2,1)} %copy-done, bf16[4,32,1024]{2,1,0:T(8,128)(2,1)} %copy-done.1, ...), custom_call_target="tpu_custom_call" | custom-call | tf_op jit(solution)/shard_map/cross/pallas_call | solution.py:334
  100.6 1.9 collective-permute-start.12
  102.5 6.6 %collective-permute-start.13 = (bf16[4,96,768]{2,1,0:T(8,128)(2,1)}, bf16[4,96,768]{2,1,0:T(8,128)(2,1)S(1)}, u32[]{:S(2)}, u32[]{:S(2)}) collective-permute-start(bf16[4,96,768]{2,1,0:T(8,128)(2,1)} %get-tuple-element.55), channel_id=1, source_target_pairs={{4,0},{8,4},{12,8},{16,12},{20,16},{24,20},{28,24},{32,28},{36,32}... | collective-permute-start | bytes 1769480 | tf_op jit(solution)/shard_map/ppermute | solution.py:517
  109.1 2.7 %tables.5 = (bf16[2,1024,256]{2,1,0:T(8,128)(2,1)}, bf16[2,1024,256]{2,1,0:T(8,128)(2,1)}) custom-call(f32[8,2,32,128]{3,2,1,0:T(8,128)} %constant.24.clone.coarse_ref, f32[8,2,32,128]{3,2,1,0:T(8,128)} %constant.25.clone.fine_ref), custom_call_target="tpu_custom_call" | custom-call | tf_op jit(solution)/shard_map/tables/pallas_call | solution.py:62
  113.4 3.1 %select.3 = (f32[4,96,768]{2,1,0:T(8,128)}, bf16[4,96,768]{2,1,0:T(8,128)(2,1)}) custom-call(s32[8]{0:T(128)} %get-tuple-element.53.sorted_ref.ordered_ref, s32[2]{0:T(128)} %pad_add_fusion.place_ref, f32[4,96,768]{2,1,0:T(8,128)} %get-tuple-element.39.own_ref, bf16[4,96,768]{2,1,0:T(8,128)(2,1)} %copy-done.14, bf16[4,96,768]{2,1,0:T(8,128)(2,1)} %copy-done.15), custom_call_target="tpu_custom_call" | custom-call | tf_op jit(solution)/shard_map/select/pallas_call | solution.py:375
  116.5 14.4 %cross.5 = (f32[4,96,512]{2,1,0:T(8,128)}, bf16[4,96,512]{2,1,0:T(8,128)(2,1)}, bf16[4,96,512]{2,1,0:T(8,128)(2,1)}) custom-call(s32[9]{0:T(128)} %pad_add_fusion.1.limits_ref, bf16[12,96,1024]{2,1,0:T(8,128)(2,1)} %normalize.2.near_ref, bf16[12,96,1024]{2,1,0:T(8,128)(2,1)} %copy-done, bf16[4,32,1024]{2,1,0:T(8,128)(2,1)} %copy-done.1, ...), custom_call_target="tpu_custom_call" | custom-call | tf_op jit(solution)/shard_map/cross/pallas_call | solution.py:334
  131.0 0.9 copy-done.12
  131.8 0.8 copy-done.13
  132.7 3.1 %select.5 = (f32[4,96,768]{2,1,0:T(8,128)}, bf16[4,96,768]{2,1,0:T(8,128)(2,1)}) custom-call(s32[8]{0:T(128)} %get-tuple-element.53.sorted_ref.ordered_ref, s32[2]{0:T(128)} %pad_add_fusion.place_ref, f32[4,96,768]{2,1,0:T(8,128)} %get-tuple-element.36.own_ref, bf16[4,96,768]{2,1,0:T(8,128)(2,1)} %copy-done.12, bf16[4,96,768]{2,1,0:T(8,128)(2,1)} %copy-done.13), custom_call_target="tpu_custom_call" | custom-call | tf_op jit(solution)/shard_map/select/pallas_call | solution.py:375
  136.0 2.0 %collective-permute-start.6 = (bf16[4,96,512]{2,1,0:T(8,128)(2,1)}, bf16[4,96,512]{2,1,0:T(8,128)(2,1)S(1)}, u32[]{:S(2)}, u32[]{:S(2)}) collective-permute-start(bf16[4,96,512]{2,1,0:T(8,128)(2,1)} %get-tuple-element.46), channel_id=1, source_target_pairs={{0,4},{4,8},{8,12},{12,16},{16,20},{20,24},{24,28},{28,32},{32,36}... | collective-permute-start | bytes 1179656 | tf_op jit(solution)/shard_map/ppermute | solution.py:517
  138.0 6.4 %collective-permute-start.7 = (bf16[4,96,512]{2,1,0:T(8,128)(2,1)S(1)}, bf16[4,96,512]{2,1,0:T(8,128)(2,1)S(1)}, u32[]{:S(2)}, u32[]{:S(2)}) collective-permute-start(bf16[4,96,512]{2,1,0:T(8,128)(2,1)S(1)} %copy-done.19), channel_id=1, source_target_pairs={{4,0},{8,4},{12,8},{16,12},{20,16},{24,20},{28,24},{32,28},{36,32}... | collective-permute-start | bytes 1179656 | tf_op jit(solution)/shard_map/ppermute | solution.py:517
  144.4 2.7 %collective-permute-start.10 = (bf16[4,96,768]{2,1,0:T(8,128)(2,1)}, bf16[4,96,768]{2,1,0:T(8,128)(2,1)S(1)}, u32[]{:S(2)}, u32[]{:S(2)}) collective-permute-start(bf16[4,96,768]{2,1,0:T(8,128)(2,1)} %get-tuple-element.51), channel_id=1, source_target_pairs={{0,2},{1,3},{2,0},{3,1},{4,6},{5,7},{6,4},{7,5},{8,10},{9,11},{10,... | collective-permute-start | bytes 1769480 | tf_op jit(solution)/shard_map/ppermute | solution.py:521
  147.1 11.3 %collective-permute-done.6.below_ref = bf16[4,96,512]{2,1,0:T(8,128)(2,1)S(1)} collective-permute-done((bf16[4,96,512]{2,1,0:T(8,128)(2,1)}, bf16[4,96,512]{2,1,0:T(8,128)(2,1)S(1)}, u32[]{:S(2)}, u32[]{:S(2)}) %collective-permute-start.6) | collective-permute-done | bytes 393248 | tf_op jit(solution)/shard_map/ppermute | solution.py:517
  159.9 2.6 %select.4 = (f32[4,96,512]{2,1,0:T(8,128)}, bf16[4,96,512]{2,1,0:T(8,128)(2,1)}) custom-call(s32[8]{0:T(128)} %get-tuple-element.53.sorted_ref.ordered_ref, s32[2]{0:T(128)} %pad_add_fusion.place_ref, f32[4,96,512]{2,1,0:T(8,128)} %get-tuple-element.45.own_ref, bf16[4,96,512]{2,1,0:T(8,128)(2,1)} %copy-done.17, bf16[4,96,512]{2,1,0:T(8,128)(2,1)} %copy-done.18), custom_call_target="tpu_custom_call" | custom-call | tf_op jit(solution)/shard_map/select/pallas_call | solution.py:375
  162.5 1.5 collective-permute-start.8
  164.3 9.6 %collective-permute-done.10 = bf16[4,96,768]{2,1,0:T(8,128)(2,1)S(1)} collective-permute-done((bf16[4,96,768]{2,1,0:T(8,128)(2,1)}, bf16[4,96,768]{2,1,0:T(8,128)(2,1)S(1)}, u32[]{:S(2)}, u32[]{:S(2)}) %collective-permute-start.10) | collective-permute-done | bytes 589856 | tf_op jit(solution)/shard_map/ppermute | solution.py:521
  174.1 7.5 %collective-permute-done.8 = bf16[4,96,512]{2,1,0:T(8,128)(2,1)S(1)} collective-permute-done((bf16[4,96,512]{2,1,0:T(8,128)(2,1)}, bf16[4,96,512]{2,1,0:T(8,128)(2,1)S(1)}, u32[]{:S(2)}, u32[]{:S(2)}) %collective-permute-start.8) | collective-permute-done | bytes 393248 | tf_op jit(solution)/shard_map/ppermute | solution.py:521
  183.1 8.5 %early.1 = (f32[384,1024]{1,0:T(8,128)}, f32[384,1024]{1,0:T(8,128)}) custom-call(s32[8]{0:T(128)} %get-tuple-element.53.sorted_ref.ordered_ref, bf16[4,96,768]{2,1,0:T(8,128)(2,1)} %copy-done.5, bf16[4,96,768]{2,1,0:T(8,128)(2,1)} %copy-done.11, bf16[3,1024,256]{2,1,0:T(8,128)(2,1)} %get-tuple-element.38.table_ref.refs_2_, ...), custom_call_target="tpu_custom_call" | custom-call | tf_op jit(solution)/shard_map/early/pallas_call | solution.py:440
  192.4 6.8 %last.1 = f32[4,96,2048]{2,1,0:T(8,128)} custom-call(s32[8]{0:T(128)} %get-tuple-element.53.sorted_ref.ordered_ref, bf16[4,96,512]{2,1,0:T(8,128)(2,1)} %copy-done.6, bf16[4,96,512]{2,1,0:T(8,128)(2,1)} %copy-done.16, bf16[2,1024,256]{2,1,0:T(8,128)(2,1)} %get-tuple-element.44.table_ref.hi_ref, bf16[2,1024,256]{2,1,0:T(8,128)(2,1)} %get-tuple-element.50.lo_ref, ...), custom_call_target="tpu_custom_call" | custom-call | tf_op jit(solution)/shard_map/last/pallas_call | solution.py:490
  (69 shorter events, 10.1 us)
Async XLA Ops:
  15.6 32.2 %collective-permute-start.3 = (bf16[12,96,1024]{2,1,0:T(8,128)(2,1)}, bf16[12,96,1024]{2,1,0:T(8,128)(2,1)S(1)}, u32[]{:S(2)}, u32[]{:S(2)}) collective-permute-start(bf16[12,96,1024]{2,1,0:T(8,128)(2,1)} %normalize.3), channel_id=1, source_target_pairs={{0,1},{1,0},{2,3},{3,2},{4,5},{5,4},{6,7},{7,6},{8,9},{9,8},{10,11... | collective-permute-start | bytes 7077896 | tf_op jit(solution)/shard_map/ppermute | solution.py:521
  20.2 1.6 collective-permute-start
  21.8 21.3 %copy-start.1 = (bf16[4,32,1024]{2,1,0:T(8,128)(2,1)}, bf16[4,32,1024]{2,1,0:T(8,128)(2,1)S(1)}, u32[]{:S(2)}) copy-start(bf16[4,32,1024]{2,1,0:T(8,128)(2,1)S(1)} %constant_dynamic-update-slice_fusion.own_src_ref) | copy-start | bytes 786436
  21.8 24.9 %collective-permute-start.2 = (bf16[4,32,1024]{2,1,0:T(8,128)(2,1)S(1)}, bf16[4,32,1024]{2,1,0:T(8,128)(2,1)S(1)}, u32[]{:S(2)}, u32[]{:S(2)}) collective-permute-start(bf16[4,32,1024]{2,1,0:T(8,128)(2,1)S(1)} %constant_dynamic-update-slice_fusion.own_src_ref), channel_id=1, source_target_pairs={{0,4},{4,8},{8,12},{12,16},{16,20},{20,24},{24,28},{28,32},{32,36}... | collective-permute-start | bytes 786440 | tf_op jit(solution)/shard_map/ppermute | solution.py:517
  25.1 21.9 %collective-permute-start.1 = (bf16[4,32,1024]{2,1,0:T(8,128)(2,1)S(1)}, bf16[4,32,1024]{2,1,0:T(8,128)(2,1)S(1)}, u32[]{:S(2)}, u32[]{:S(2)}) collective-permute-start(bf16[4,32,1024]{2,1,0:T(8,128)(2,1)S(1)} %constant_dynamic-update-slice_fusion.own_src_ref), channel_id=1, source_target_pairs={{4,0},{8,4},{12,8},{16,12},{20,16},{24,20},{28,24},{32,28},{36,32}... | collective-permute-start | bytes 786440 | tf_op jit(solution)/shard_map/ppermute | solution.py:517
  46.8 1.0 copy-start.2
  47.0 0.9 copy-start.3
  47.8 1.4 copy-start
  68.9 43.4 %collective-permute-start.4 = (bf16[4,96,768]{2,1,0:T(8,128)(2,1)}, bf16[4,96,768]{2,1,0:T(8,128)(2,1)S(1)}, u32[]{:S(2)}, u32[]{:S(2)}) collective-permute-start(bf16[4,96,768]{2,1,0:T(8,128)(2,1)} %get-tuple-element.40), channel_id=1, source_target_pairs={{0,4},{4,8},{8,12},{12,16},{16,20},{20,24},{24,28},{28,32},{32,36}... | collective-permute-start | bytes 1769480 | tf_op jit(solution)/shard_map/ppermute | solution.py:517
  70.8 41.5 %collective-permute-start.5 = (bf16[4,96,768]{2,1,0:T(8,128)(2,1)}, bf16[4,96,768]{2,1,0:T(8,128)(2,1)S(1)}, u32[]{:S(2)}, u32[]{:S(2)}) collective-permute-start(bf16[4,96,768]{2,1,0:T(8,128)(2,1)} %get-tuple-element.41), channel_id=1, source_target_pairs={{4,0},{8,4},{12,8},{16,12},{20,16},{24,20},{28,24},{32,28},{36,32}... | collective-permute-start | bytes 1769480 | tf_op jit(solution)/shard_map/ppermute | solution.py:517
  100.6 30.3 %collective-permute-start.12 = (bf16[4,96,768]{2,1,0:T(8,128)(2,1)}, bf16[4,96,768]{2,1,0:T(8,128)(2,1)S(1)}, u32[]{:S(2)}, u32[]{:S(2)}) collective-permute-start(bf16[4,96,768]{2,1,0:T(8,128)(2,1)} %get-tuple-element.54), channel_id=1, source_target_pairs={{0,4},{4,8},{8,12},{12,16},{16,20},{20,24},{24,28},{28,32},{32,36}... | collective-permute-start | bytes 1769480 | tf_op jit(solution)/shard_map/ppermute | solution.py:517
  102.5 28.4 %collective-permute-start.13 = (bf16[4,96,768]{2,1,0:T(8,128)(2,1)}, bf16[4,96,768]{2,1,0:T(8,128)(2,1)S(1)}, u32[]{:S(2)}, u32[]{:S(2)}) collective-permute-start(bf16[4,96,768]{2,1,0:T(8,128)(2,1)} %get-tuple-element.55), channel_id=1, source_target_pairs={{4,0},{8,4},{12,8},{16,12},{20,16},{24,20},{28,24},{32,28},{36,32}... | collective-permute-start | bytes 1769480 | tf_op jit(solution)/shard_map/ppermute | solution.py:517
  112.4 0.8 copy-start.14
  112.4 1.0 copy-start.15
  130.9 7.1 %copy-start.19 = (bf16[4,96,512]{2,1,0:T(8,128)(2,1)S(1)}, bf16[4,96,512]{2,1,0:T(8,128)(2,1)}, u32[]{:S(2)}) copy-start(bf16[4,96,512]{2,1,0:T(8,128)(2,1)} %get-tuple-element.47) | copy-start | bytes 1179652
  131.0 0.9 copy-start.12
  131.8 0.8 copy-start.13
  135.8 28.3 %copy-start.8 = (f32[4,96,768]{2,1,0:T(8,128)S(1)}, f32[4,96,768]{2,1,0:T(8,128)}, u32[]{:S(2)}) copy-start(f32[4,96,768]{2,1,0:T(8,128)} %get-tuple-element.56) | copy-start | bytes 3538948
  135.8 28.3 %collective-permute-start.14 = (bf16[4,96,768]{2,1,0:T(8,128)(2,1)}, bf16[4,96,768]{2,1,0:T(8,128)(2,1)S(1)}, u32[]{:S(2)}, u32[]{:S(2)}) collective-permute-start(bf16[4,96,768]{2,1,0:T(8,128)(2,1)} %get-tuple-element.57), channel_id=1, source_target_pairs={{0,2},{1,3},{2,0},{3,1},{4,6},{5,7},{6,4},{7,5},{8,10},{9,11},{10,... | collective-permute-start | bytes 1769480 | tf_op jit(solution)/shard_map/ppermute | solution.py:521
  136.0 22.4 %collective-permute-start.6 = (bf16[4,96,512]{2,1,0:T(8,128)(2,1)}, bf16[4,96,512]{2,1,0:T(8,128)(2,1)S(1)}, u32[]{:S(2)}, u32[]{:S(2)}) collective-permute-start(bf16[4,96,512]{2,1,0:T(8,128)(2,1)} %get-tuple-element.46), channel_id=1, source_target_pairs={{0,4},{4,8},{8,12},{12,16},{16,20},{20,24},{24,28},{28,32},{32,36}... | collective-permute-start | bytes 1179656 | tf_op jit(solution)/shard_map/ppermute | solution.py:517
  138.0 20.3 %collective-permute-start.7 = (bf16[4,96,512]{2,1,0:T(8,128)(2,1)S(1)}, bf16[4,96,512]{2,1,0:T(8,128)(2,1)S(1)}, u32[]{:S(2)}, u32[]{:S(2)}) collective-permute-start(bf16[4,96,512]{2,1,0:T(8,128)(2,1)S(1)} %copy-done.19), channel_id=1, source_target_pairs={{4,0},{8,4},{12,8},{16,12},{20,16},{24,20},{28,24},{32,28},{36,32}... | collective-permute-start | bytes 1179656 | tf_op jit(solution)/shard_map/ppermute | solution.py:517
  144.4 29.5 %collective-permute-start.10 = (bf16[4,96,768]{2,1,0:T(8,128)(2,1)}, bf16[4,96,768]{2,1,0:T(8,128)(2,1)S(1)}, u32[]{:S(2)}, u32[]{:S(2)}) collective-permute-start(bf16[4,96,768]{2,1,0:T(8,128)(2,1)} %get-tuple-element.51), channel_id=1, source_target_pairs={{0,2},{1,3},{2,0},{3,1},{4,6},{5,7},{6,4},{7,5},{8,10},{9,11},{10,... | collective-permute-start | bytes 1769480 | tf_op jit(solution)/shard_map/ppermute | solution.py:521
  162.5 11.4 %copy-start.7 = (f32[4,96,768]{2,1,0:T(8,128)S(1)}, f32[4,96,768]{2,1,0:T(8,128)}, u32[]{:S(2)}) copy-start(f32[4,96,768]{2,1,0:T(8,128)} %get-tuple-element.42) | copy-start | bytes 3538948
  162.5 19.1 %collective-permute-start.8 = (bf16[4,96,512]{2,1,0:T(8,128)(2,1)}, bf16[4,96,512]{2,1,0:T(8,128)(2,1)S(1)}, u32[]{:S(2)}, u32[]{:S(2)}) collective-permute-start(bf16[4,96,512]{2,1,0:T(8,128)(2,1)} %get-tuple-element.49), channel_id=1, source_target_pairs={{0,2},{1,3},{2,0},{3,1},{4,6},{5,7},{6,4},{7,5},{8,10},{9,11},{10,... | collective-permute-start | bytes 1179656 | tf_op jit(solution)/shard_map/ppermute | solution.py:521
  164.1 17.6 %copy-start.4 = (bf16[4,96,768]{2,1,0:T(8,128)(2,1)}, bf16[4,96,768]{2,1,0:T(8,128)(2,1)S(1)}, u32[]{:S(2)}) copy-start(bf16[4,96,768]{2,1,0:T(8,128)(2,1)S(1)} %add_convert_fusion.refs_4_) | copy-start | bytes 1769476
  164.2 17.4 %copy-start.9 = (f32[4,96,512]{2,1,0:T(8,128)S(1)}, f32[4,96,512]{2,1,0:T(8,128)}, u32[]{:S(2)}) copy-start(f32[4,96,512]{2,1,0:T(8,128)} %get-tuple-element.48) | copy-start | bytes 2359300
  164.2 17.9 %collective-permute-start.15 = (bf16[4,96,768]{2,1,0:T(8,128)(2,1)S(1)}, bf16[4,96,768]{2,1,0:T(8,128)(2,1)S(1)}, u32[]{:S(2)}, u32[]{:S(2)}) collective-permute-start(bf16[4,96,768]{2,1,0:T(8,128)(2,1)S(1)} %add_convert_fusion.refs_4_), channel_id=1, source_target_pairs={{0,1},{1,0},{2,3},{3,2},{4,5},{5,4},{6,7},{7,6},{8,9},{9,8},{10,11... | collective-permute-start | bytes 1769480 | tf_op jit(solution)/shard_map/ppermute | solution.py:521
  174.0 8.1 %copy-start.5 = (bf16[4,96,768]{2,1,0:T(8,128)(2,1)}, bf16[4,96,768]{2,1,0:T(8,128)(2,1)S(1)}, u32[]{:S(2)}) copy-start(bf16[4,96,768]{2,1,0:T(8,128)(2,1)S(1)} %add_convert_fusion.1.refs_0_) | copy-start | bytes 1769476
  174.0 8.1 %collective-permute-start.11 = (bf16[4,96,768]{2,1,0:T(8,128)(2,1)S(1)}, bf16[4,96,768]{2,1,0:T(8,128)(2,1)S(1)}, u32[]{:S(2)}, u32[]{:S(2)}) collective-permute-start(bf16[4,96,768]{2,1,0:T(8,128)(2,1)S(1)} %add_convert_fusion.1.refs_0_), channel_id=1, source_target_pairs={{0,1},{1,0},{2,3},{3,2},{4,5},{5,4},{6,7},{7,6},{8,9},{9,8},{10,11... | collective-permute-start | bytes 1769480 | tf_op jit(solution)/shard_map/ppermute | solution.py:521
  181.7 9.9 %copy-start.6 = (bf16[4,96,512]{2,1,0:T(8,128)(2,1)}, bf16[4,96,512]{2,1,0:T(8,128)(2,1)S(1)}, u32[]{:S(2)}) copy-start(bf16[4,96,512]{2,1,0:T(8,128)(2,1)S(1)} %add_convert_fusion.2.mine_ref) | copy-start | bytes 1179652
  181.7 9.9 %collective-permute-start.9 = (bf16[4,96,512]{2,1,0:T(8,128)(2,1)S(1)}, bf16[4,96,512]{2,1,0:T(8,128)(2,1)S(1)}, u32[]{:S(2)}, u32[]{:S(2)}) collective-permute-start(bf16[4,96,512]{2,1,0:T(8,128)(2,1)S(1)} %add_convert_fusion.2.mine_ref), channel_id=1, source_target_pairs={{0,1},{1,0},{2,3},{3,2},{4,5},{5,4},{6,7},{7,6},{8,9},{9,8},{10,11... | collective-permute-start | bytes 1179656 | tf_op jit(solution)/shard_map/ppermute | solution.py:521
  182.1 1.0 copy-start.11
  (4 other events, 3.1 us)

commit v3 on v2

--- a/solution.py
+++ b/solution.py
@@ -9,6 +9,7 @@
 from jax.experimental.pallas import tpu as pltpu
 from jax.sharding import PartitionSpec as P
 
+
 SEG = 1024
 HALF = 96
 LANES = 128
@@ -16,6 +17,7 @@
 PAIR = 2 * LANES
 CHUNKS = ((0, 3), (3, 3), (6, 2))
 FOLD = 32
+UNROLL = 4
 TILE = 32
 SUB = 16
 PITCH = 104
@@ -40,19 +42,23 @@
     fine_cos = fine_ref[0, 0]
     fine_sin = fine_ref[0, 1]
 
-    def row_block(a, carry):
-        base_cos = jnp.concatenate([coarse_ref[0, 0, pl.ds(a, 8, stride=0), :]] * (FOLD // 8), axis=0)
-        base_sin = jnp.concatenate([coarse_ref[0, 1, pl.ds(a, 8, stride=0), :]] * (FOLD // 8), axis=0)
-        real = base_cos * fine_cos - base_sin * fine_sin
-        imag = -(base_sin * fine_cos + base_cos * fine_sin)
-        rows = pl.ds(pl.multiple_of(a * FOLD, FOLD), FOLD)
-        for part, lane in ((real, 0), (imag, LANES)):
-            top = part.astype(jnp.bfloat16)
-            hi_ref[0, rows, lane:lane + LANES] = top
-            lo_ref[0, rows, lane:lane + LANES] = (part - top.astype(jnp.float32)).astype(jnp.bfloat16)
+    def row_block(step, carry):
+        for inner in range(UNROLL):
+            a = step * UNROLL + inner
+            base_cos = coarse_ref[0, 0, pl.ds(a, 8, stride=0), :]
+            base_sin = coarse_ref[0, 1, pl.ds(a, 8, stride=0), :]
+            base_cos = jnp.concatenate([base_cos] * (FOLD // 8), axis=0)
+            base_sin = jnp.concatenate([base_sin] * (FOLD // 8), axis=0)
+            real = base_cos * fine_cos - base_sin * fine_sin
+            imag = -(base_sin * fine_cos + base_cos * fine_sin)
+            rows = pl.ds(pl.multiple_of(a * FOLD, FOLD), FOLD)
+            for part, lane in ((real, 0), (imag, LANES)):
+                top = part.astype(jnp.bfloat16)
+                hi_ref[0, rows, lane:lane + LANES] = top
+                lo_ref[0, rows, lane:lane + LANES] = (part - top.astype(jnp.float32)).astype(jnp.bfloat16)
         return carry
 
-    lax.fori_loop(0, FOLD, row_block, 0)
+    lax.fori_loop(0, FOLD // UNROLL, row_block, 0)
 
 
 def make_tables(first, count, coarse, fine):
@@ -69,7 +75,8 @@
     )(coarse, fine)
 
 
-def normalize_kernel(half_ref, samples_ref, scale_ref, out_ref, buffer_ref, sems, *, seg_count, windows):
+def normalize_kernel(half_ref, samples_ref, scale_ref, out_ref, buffer_ref, spread_ref, wide_ref, sems, *,
+                     seg_count, windows):
     step = pl.program_id(0)
     steps = pl.num_programs(0)
     per_channel = samples_ref.shape[1]
@@ -94,6 +101,23 @@
     def _():
         copy(step + 1, 1 - slot).start()
 
+    columns = wide_ref.shape[0]
+
+    @pl.when(step == 0)
+    def _():
+        for column in range(columns):
+            row = lax.broadcasted_iota(jnp.int32, (columns, LANES), 0)
+            spread_ref[:, column * LANES:(column + 1) * LANES] = jnp.where(row == column, 1.0, 0.0).astype(jnp.bfloat16)
+
+    scale = scale_ref[...]
+    narrow = scale[:, :columns].astype(jnp.bfloat16)
+    for column in range(0, columns, 2):
+        both = jnp.dot(
+            narrow, spread_ref[:, column * LANES:(column + 2) * LANES], preferred_element_type=jnp.float32
+        )
+        wide_ref[column] = both[:, :LANES]
+        wide_ref[column + 1] = both[:, LANES:]
+
     copy(step, slot).wait()
     flat = buffer_ref.reshape(2 * TILE * PITCH, LANES)
     base = slot * (TILE * PITCH)
@@ -102,7 +126,6 @@
         start = base + (n * pieces + piece) * windows + w
         return flat[pl.ds(start, TILE, stride=PITCH), :].astype(jnp.float32)
 
-    scale = scale_ref[...]
     live = scale[:, windows * blocks:windows * blocks + 1]
     for w in range(windows):
         total = jnp.zeros((TILE, LANES), jnp.float32)
@@ -111,14 +134,14 @@
                 column = w * blocks + n * pairs + pair
                 one = rows(w, n, 2 * pair)
                 two = rows(w, n, 2 * pair + 1)
-                weight = scale[:, column:column + 1]
+                weight = wide_ref[column]
                 total = total + (one * one + two * two) * (weight * weight)
         energy = jnp.sum(total, axis=1, keepdims=True) * (1.0 / (seg_count * SEG))
-        factor = live * lax.rsqrt(energy + 1e-06)
+        factor = jnp.broadcast_to(live * lax.rsqrt(energy + 1e-06), (TILE, LANES))
         for n in range(seg_count):
             for pair in range(pairs):
                 column = w * blocks + n * pairs + pair
-                weight = scale[:, column:column + 1] * factor
+                weight = wide_ref[column] * factor
                 for piece in (2 * pair, 2 * pair + 1):
                     value = rows(w, n, piece) * weight
                     out_ref[w * seg_count + n, :, piece * LANES:(piece + 1) * LANES] = value.astype(jnp.bfloat16)
@@ -138,6 +161,8 @@
             out_specs=pl.BlockSpec((windows * seg_count, TILE, SEG), lambda i, h: (0, i, 0)),
             scratch_shapes=[
                 pltpu.VMEM((2, TILE, PITCH, LANES), jnp.int32),
+                pltpu.VMEM((scales.shape[1] - 1, (scales.shape[1] - 1) * LANES), jnp.bfloat16),
+                pltpu.VMEM((scales.shape[1] - 1, TILE, LANES), jnp.float32),
                 pltpu.SemaphoreType.DMA((2,)),
             ],
         ),
@@ -151,7 +176,6 @@
     pieces = SEG // LANES
     pairs = pieces // 2
     blocks = seg_count * pairs
-    channels = scale_ref.shape[0]
     per_channel = samples_ref.shape[1]
     given = [offsets_ref[j] for j in range(SOURCES)]
     ranks = []
@@ -354,31 +378,10 @@
     )(limits, near, far, own_src, above_src, below_src, table)
 
 
-def select_kernel(sorted_ref, place_ref, own_ref, below_ref, above_ref, kept_ref, passed_ref):
-    base = place_ref[0]
-    lower = place_ref[1] == 0
-    index = base + lax.broadcasted_iota(jnp.int32, (HALF, LANES), 0)
-    for j in range(SOURCES):
-        below_source = index < sorted_ref[j]
-        first = jnp.where(below_source, 1, 0)
-        keep = first == jnp.where(lower, 1, 0)
-        for lane in range(0, own_ref.shape[2], LANES):
-            at = (j, slice(None), slice(lane, lane + LANES))
-            own = own_ref[at]
-            other = jnp.where(below_source, above_ref[at].astype(jnp.float32), below_ref[at].astype(jnp.float32))
-            kept_ref[at] = jnp.where(keep, own, other)
-            passed_ref[at] = jnp.where(keep, other, own).astype(jnp.bfloat16)
-
-
-def select_rows(ordered, place, own, from_below, from_above):
-    whole = pl.BlockSpec(memory_space=pltpu.VMEM)
-    return pl.pallas_call(
-        select_kernel,
-        in_specs=[pl.BlockSpec(memory_space=pltpu.SMEM), pl.BlockSpec(memory_space=pltpu.SMEM), whole, whole, whole],
-        out_specs=[whole, whole],
-        out_shape=[jax.ShapeDtypeStruct(own.shape, jnp.float32), jax.ShapeDtypeStruct(own.shape, jnp.bfloat16)],
-        name="select",
-    )(ordered, place, own, from_below, from_above)
+def select_rows(below_source, keep, own, from_below, from_above):
+    other = jnp.where(below_source, from_above, from_below)
+    kept = jnp.where(keep, own, other.astype(jnp.float32))
+    return kept, jnp.where(keep, other, own.astype(jnp.bfloat16))
 
 
 def turned(ordered_ref, mine_ref, mate_ref, top_ref, halve):
@@ -409,12 +412,14 @@
 
 def early_kernel(ordered_ref, *refs, firsts):
     count = len(firsts)
+    even_ref, odd_ref = refs[4 * count:4 * count + 2]
     tops = refs[4 * count + 2:]
-    even_ref, odd_ref = refs[4 * count:4 * count + 2]
-    for c, first in enumerate(firsts):
-        @pl.when(pl.program_id(0) == 0)
-        def _():
+
+    @pl.when(pl.program_id(0) == 0)
+    def _():
+        for c, first in enumerate(firsts):
             turned(ordered_ref, refs[4 * c], refs[4 * c + 1], tops[c], first == 0)
+
     sums = [None, None]
     for c, first in enumerate(firsts):
         folded(tops[c], refs[4 * c + 2], refs[4 * c + 3], first, sums)
@@ -521,11 +526,7 @@
     return lax.ppermute(block, "win", [(i, i ^ bit) for i in range(lax.axis_size("win"))])
 
 
-def after(value, *others):
-    return lax.optimization_barrier((value,) + others)[0]
-
-
-def shards(samples, exponents, alive, offsets):
+def pipeline(samples, exponents, alive, offsets):
     channels, windows, length = samples.shape
     seg_count = length // SEG
     place = lax.axis_index("win")
@@ -538,7 +539,8 @@
     scales = jnp.concatenate([scales, alive.astype(jnp.float32).reshape(channels, 1)], axis=1)
 
     own_src, ordered = source_rows(offsets, samples_rows, scales, seg_count, windows)
-    own_src = jnp.concatenate([own_src, partner(own_src, 1)], axis=1)
+    mate_src = partner(own_src, 1)
+    own_src = jnp.concatenate([own_src, mate_src], axis=1)
     above_src = passed_along(own_src, "chan", -1)
     below_src = passed_along(own_src, "chan", 1)
 
@@ -553,33 +555,39 @@
     limits = jnp.concatenate(
         [(core * HALF).reshape(1), jnp.where(above_off == 0, channels, above_off - 1), below_off - 1]
     ).astype(jnp.int32)
-    where_am_i = jnp.stack([core * HALF, upper_half]).astype(jnp.int32)
+    index = core * HALF + jnp.arange(HALF, dtype=jnp.int32)
+    below_source = (index[None, :] < ordered[:SOURCES, None])[:, :, None]
+    keep = below_source == (upper_half == 0)
     scale = 2.0 / float(2 * SEG * windows * lax.axis_size("win") * seg_count * SEG)
 
-    tables = [make_tables(first, count, coarse, fine) for first, count in CHUNKS]
-    total_chunks = len(CHUNKS)
-    crossed, returned, selected, parts = [], [], [], []
-
-    def finish(c):
+    tables = []
+    for first, count in CHUNKS:
+        tables.append(make_tables(first, count, coarse, fine))
+    crossed, returned, selected = [], [], []
+
+    def select(c):
+        pieces = (crossed[c],) + returned[c]
+        if c:
+            pieces = lax.optimization_barrier(pieces + (selected[c - 1][0],))[:3]
+        kept, moved = select_rows(below_source, keep, *pieces)
+        selected.append((kept, partner(moved, 2)))
+
+    for c in range(len(CHUNKS)):
+        own, to_above, to_below = cross_chunk(limits, near, far, own_src, above_src, below_src, tables[c][0])
+        crossed.append(own)
+        from_below = passed_along(to_above, "chan", 1)
+        from_above = passed_along(to_below, "chan", -1)
+        returned.append((from_below, from_above))
+    for c in range(len(CHUNKS)):
+        select(c)
+    parts = []
+    for c in range(len(CHUNKS)):
         kept, moved = selected[c]
+        if c:
+            kept = lax.optimization_barrier((kept, parts[c - 1][0]))[0]
         total = (kept + moved.astype(jnp.float32)).astype(jnp.bfloat16)
-        parts.append((total, partner(total, 1)) + tuple(tables[c]))
-
-    for c in range(total_chunks):
-        gate = limits
-        if c >= 2:
-            gate = after(limits, selected[c - 2][0])
-        own, to_above, to_below = cross_chunk(gate, near, far, own_src, above_src, below_src, tables[c][0])
-        crossed.append(own)
-        returned.append((passed_along(to_above, "chan", 1), passed_along(to_below, "chan", -1)))
-        if c >= 1:
-            kept, moved = select_rows(after(ordered, own), where_am_i, crossed[c - 1], *returned[c - 1])
-            selected.append((kept, partner(moved, 2)))
-    c = total_chunks - 1
-    kept, moved = select_rows(ordered, where_am_i, crossed[c], *returned[c])
-    selected.append((kept, partner(moved, 2)))
-    for c in range(total_chunks):
-        finish(c)
+        mate = partner(total, 1)
+        parts.append((total, mate) + tuple(tables[c]))
     firsts = tuple(first for first, _ in CHUNKS)
     even, odd = early_inverse(ordered, parts[:-1], firsts[:-1])
     return last_inverse(ordered, parts[-1], even, odd, firsts[-1], scale)
@@ -587,6 +595,4 @@
 
 def solution(mesh):
     placed = (P("chan", "win", None), P("chan", "win", None), P("chan"), P("chan"))
-    return jax.shard_map(
-        shards, mesh=mesh, in_specs=placed, out_specs=P("chan", "win", None), check_vma=False
-    )
+    return jax.shard_map(pipeline, mesh=mesh, in_specs=placed, out_specs=P("chan", "win", None), check_vma=False)

time: 200 us -> 185 us (0.925)
  the two profiles are of different devices: /device:TPU:69 before, /device:TPU:37 now
where the time goes in v3:
time: 185 us; the launch traced here: 182 us
  Pallas kernels  90.1 us (49%)
  starting transfers between devices  63 us (34%)
  waiting for transfers between devices  16 us (9%)
  other arithmetic  8.39 us (5%)
  local copies, waits for them, and re-layouts  4.3 us (2%)
    pallas_call x3, Pallas kernels, cross_chunk(): pl.pallas_call(cross_kernel, grid_spec=pltpu.PrefetchScalarGridSpec(num_s...  49.5 us
    ppermute x8, starting transfers between devices, partner(): lax.ppermute(block, 'win', [(i, i ^ bit) for i in range(lax.axis_size('wi...  32.3 us
    ppermute x8, starting transfers between devices, passed_along(): return lax.ppermute(block, axis, route)  30.7 us
    ppermute x8, waiting for transfers between devices, passed_along(): return lax.ppermute(block, axis, route)  15.4 us
    pallas_call x2, Pallas kernels, normalize_half(): pl.pallas_call(functools.partial(normalize_kernel, seg_count=seg_count, w...  12.1 us
    pallas_call x3, Pallas kernels, make_tables(): pl.pallas_call(table_kernel, grid=(count,), in_specs=[small, small], out_...  9.39 us
    pallas_call x1, Pallas kernels, early_inverse(): pl.pallas_call(functools.partial(early_kernel, firsts=firsts), grid_spec=...  8.47 us
    pallas_call x1, Pallas kernels, last_inverse(): pl.pallas_call(functools.partial(last_kernel, first=first, scale=scale),...  6.76 us
  transfers between devices with their start and end apart: 16, of which 3 were waited for; matrix products, arithmetic and copies ran while one was open for 3% of the time, Pallas kernels for 32%

profile of v3, /device:TPU:37, one launch (start us, length us, event | category | flops | bytes accessed | tf_op | source)
XLA Modules:
  0.0 182.3 jit_solution(8320930863686309625)
XLA Ops:
  0.0 0.9 select_reduce_fusion
  2.6 6.1 %normalize.3 = bf16[12,96,1024]{2,1,0:T(8,128)(2,1)} custom-call(s32[1]{0:T(128)} %bitcast.9.half_ref, s32[192,96,128]{2,1,0:T(8,128)} %bitcast.11, f32[192,49]{1,0:T(8,128)} %pad_maximum_fusion.scale_ref), custom_call_target="tpu_custom_call" | custom-call | tf_op jit(solution)/shard_map/normalize/pallas_call | solution.py:152
  9.4 3.8 %sources.1 = (bf16[4,16,1024]{2,1,0:T(8,128)(2,1)}, s32[8]{0:T(128)}) custom-call(s32[4]{0:T(128)} %offsets_ref.1, s32[192,96,128]{2,1,0:T(8,128)} %bitcast.12, f32[192,49]{1,0:T(8,128)} %pad_maximum_fusion.scale_ref), custom_call_target="tpu_custom_call" | custom-call | tf_op jit(solution)/shard_map/sources/pallas_call | solution.py:241
  13.3 0.9 constant_dynamic-update-slice_fusion.1
  14.9 3.2 %collective-permute-start.2 = (bf16[4,32,1024]{2,1,0:T(8,128)(2,1)S(1)}, bf16[4,32,1024]{2,1,0:T(8,128)(2,1)S(1)}, u32[]{:S(2)}, u32[]{:S(2)}) collective-permute-start(bf16[4,32,1024]{2,1,0:T(8,128)(2,1)S(1)} %constant_dynamic-update-slice_fusion.own_src_ref), channel_id=1, source_target_pairs={{0,4},{4,8},{8,12},{12,16},{16,20},{20,24},{24,28},{28,32},{32,36}... | collective-permute-start | bytes 786440 | tf_op jit(solution)/shard_map/ppermute | solution.py:522
  18.1 5.1 %collective-permute-start.1 = (bf16[4,32,1024]{2,1,0:T(8,128)(2,1)S(1)}, bf16[4,32,1024]{2,1,0:T(8,128)(2,1)S(1)}, u32[]{:S(2)}, u32[]{:S(2)}) collective-permute-start(bf16[4,32,1024]{2,1,0:T(8,128)(2,1)S(1)} %constant_dynamic-update-slice_fusion.own_src_ref), channel_id=1, source_target_pairs={{4,0},{8,4},{12,8},{16,12},{20,16},{24,20},{28,24},{32,28},{36,32}... | collective-permute-start | bytes 786440 | tf_op jit(solution)/shard_map/ppermute | solution.py:522
  23.2 6.1 %normalize.2.near_ref = bf16[12,96,1024]{2,1,0:T(8,128)(2,1)} custom-call(s32[1]{0:T(128)} %bitcast.6.half_ref, s32[192,96,128]{2,1,0:T(8,128)} %bitcast.13, f32[192,49]{1,0:T(8,128)} %pad_maximum_fusion.scale_ref), custom_call_target="tpu_custom_call" | custom-call | tf_op jit(solution)/shard_map/normalize/pallas_call | solution.py:152
  29.3 3.4 %tables.5 = (bf16[3,1024,256]{2,1,0:T(8,128)(2,1)}, bf16[3,1024,256]{2,1,0:T(8,128)(2,1)}) custom-call(f32[8,2,32,128]{3,2,1,0:T(8,128)} %constant.25.clone.coarse_ref, f32[8,2,32,128]{3,2,1,0:T(8,128)} %constant.26.clone.fine_ref), custom_call_target="tpu_custom_call" | custom-call | tf_op jit(solution)/shard_map/tables/pallas_call | solution.py:68
  33.8 1.4 copy-done
  35.2 18.1 %cross.5 = (f32[4,96,768]{2,1,0:T(8,128)}, bf16[4,96,768]{2,1,0:T(8,128)(2,1)}, bf16[4,96,768]{2,1,0:T(8,128)(2,1)}) custom-call(s32[9]{0:T(128)} %pad_add_fusion.limits_ref, bf16[12,96,1024]{2,1,0:T(8,128)(2,1)} %normalize.2.near_ref, bf16[12,96,1024]{2,1,0:T(8,128)(2,1)} %copy-done, bf16[4,32,1024]{2,1,0:T(8,128)(2,1)} %copy-done.3, ...), custom_call_target="tpu_custom_call" | custom-call | tf_op jit(solution)/shard_map/cross/pallas_call | solution.py:358
  53.3 3.6 %collective-permute-start.8 = (bf16[4,96,768]{2,1,0:T(8,128)(2,1)}, bf16[4,96,768]{2,1,0:T(8,128)(2,1)S(1)}, u32[]{:S(2)}, u32[]{:S(2)}) collective-permute-start(bf16[4,96,768]{2,1,0:T(8,128)(2,1)} %get-tuple-element.44), channel_id=1, source_target_pairs={{4,0},{8,4},{12,8},{16,12},{20,16},{24,20},{28,24},{32,28},{36,32}... | collective-permute-start | bytes 1769480 | tf_op jit(solution)/shard_map/ppermute | solution.py:522
  56.9 1.9 %collective-permute-start.9 = (bf16[4,96,768]{2,1,0:T(8,128)(2,1)}, bf16[4,96,768]{2,1,0:T(8,128)(2,1)S(1)}, u32[]{:S(2)}, u32[]{:S(2)}) collective-permute-start(bf16[4,96,768]{2,1,0:T(8,128)(2,1)} %get-tuple-element.45), channel_id=1, source_target_pairs={{0,4},{4,8},{8,12},{12,16},{16,20},{20,24},{24,28},{28,32},{32,36}... | collective-permute-start | bytes 1769480 | tf_op jit(solution)/shard_map/ppermute | solution.py:522
  58.9 9.3 %collective-permute-done.8 = bf16[4,96,768]{2,1,0:T(8,128)(2,1)S(1)} collective-permute-done((bf16[4,96,768]{2,1,0:T(8,128)(2,1)}, bf16[4,96,768]{2,1,0:T(8,128)(2,1)S(1)}, u32[]{:S(2)}, u32[]{:S(2)}) %collective-permute-start.8) | collective-permute-done | bytes 589856 | tf_op jit(solution)/shard_map/ppermute | solution.py:522
  68.2 6.1 %collective-permute-done.9 = bf16[4,96,768]{2,1,0:T(8,128)(2,1)S(1)} collective-permute-done((bf16[4,96,768]{2,1,0:T(8,128)(2,1)}, bf16[4,96,768]{2,1,0:T(8,128)(2,1)S(1)}, u32[]{:S(2)}, u32[]{:S(2)}) %collective-permute-start.9) | collective-permute-done | bytes 589856 | tf_op jit(solution)/shard_map/ppermute | solution.py:522
  74.3 2.3 %convert_select_fusion.4 = bf16[4,96,768]{2,1,0:T(8,128)(2,1)} fusion(f32[4,96,768]{2,1,0:T(8,128)} %get-tuple-element.43, pred[4,96]{1,0:T(4,128)(4,1)S(1)} %get-tuple-element.61, bf16[4,96,768]{2,1,0:T(8,128)(2,1)S(1)} %collective-permute-done.8, bf16[4,96,768]{2,1,0:T(8,128)(2,1)S(1)} %collective-permute-done.9, pred[4,96]{1,0:T(4,128)(4,1)S(1)} %get-tuple-element.62), kind=kLoop, calls=%fused_computation.7 | loop fusion | flops 884736 | bytes 2949888 | tf_op jit(solution)/shard_map/jit(_where)/select_n | solution.py:384
  76.9 3.4 %tables.4 = (bf16[3,1024,256]{2,1,0:T(8,128)(2,1)}, bf16[3,1024,256]{2,1,0:T(8,128)(2,1)}) custom-call(f32[8,2,32,128]{3,2,1,0:T(8,128)} %constant.25.clone.coarse_ref, f32[8,2,32,128]{3,2,1,0:T(8,128)} %constant.26.clone.fine_ref), custom_call_target="tpu_custom_call" | custom-call | tf_op jit(solution)/shard_map/tables/pallas_call | solution.py:68
  80.3 18.0 %cross.4 = (f32[4,96,768]{2,1,0:T(8,128)}, bf16[4,96,768]{2,1,0:T(8,128)(2,1)}, bf16[4,96,768]{2,1,0:T(8,128)(2,1)}) custom-call(s32[9]{0:T(128)} %pad_add_fusion.limits_ref, bf16[12,96,1024]{2,1,0:T(8,128)(2,1)} %normalize.2.near_ref, bf16[12,96,1024]{2,1,0:T(8,128)(2,1)} %copy-done, bf16[4,32,1024]{2,1,0:T(8,128)(2,1)} %copy-done.3, ...), custom_call_target="tpu_custom_call" | custom-call | tf_op jit(solution)/shard_map/cross/pallas_call | solution.py:358
  98.3 1.9 %collective-permute-start.6 = (bf16[4,96,768]{2,1,0:T(8,128)(2,1)}, bf16[4,96,768]{2,1,0:T(8,128)(2,1)S(1)}, u32[]{:S(2)}, u32[]{:S(2)}) collective-permute-start(bf16[4,96,768]{2,1,0:T(8,128)(2,1)} %get-tuple-element.40), channel_id=1, source_target_pairs={{0,4},{4,8},{8,12},{12,16},{16,20},{20,24},{24,28},{28,32},{32,36}... | collective-permute-start | bytes 1769480 | tf_op jit(solution)/shard_map/ppermute | solution.py:522
  100.2 6.4 %collective-permute-start.7 = (bf16[4,96,768]{2,1,0:T(8,128)(2,1)}, bf16[4,96,768]{2,1,0:T(8,128)(2,1)S(1)}, u32[]{:S(2)}, u32[]{:S(2)}) collective-permute-start(bf16[4,96,768]{2,1,0:T(8,128)(2,1)} %get-tuple-element.41), channel_id=1, source_target_pairs={{4,0},{8,4},{12,8},{16,12},{20,16},{24,20},{28,24},{32,28},{36,32}... | collective-permute-start | bytes 1769480 | tf_op jit(solution)/shard_map/ppermute | solution.py:522
  106.6 2.6 %tables.3 = (bf16[2,1024,256]{2,1,0:T(8,128)(2,1)}, bf16[2,1024,256]{2,1,0:T(8,128)(2,1)}) custom-call(f32[8,2,32,128]{3,2,1,0:T(8,128)} %constant.25.clone.coarse_ref, f32[8,2,32,128]{3,2,1,0:T(8,128)} %constant.26.clone.fine_ref), custom_call_target="tpu_custom_call" | custom-call | tf_op jit(solution)/shard_map/tables/pallas_call | solution.py:68
  109.1 13.4 %cross.3 = (f32[4,96,512]{2,1,0:T(8,128)}, bf16[4,96,512]{2,1,0:T(8,128)(2,1)}, bf16[4,96,512]{2,1,0:T(8,128)(2,1)}) custom-call(s32[9]{0:T(128)} %pad_add_fusion.limits_ref, bf16[12,96,1024]{2,1,0:T(8,128)(2,1)} %normalize.2.near_ref, bf16[12,96,1024]{2,1,0:T(8,128)(2,1)} %copy-done, bf16[4,32,1024]{2,1,0:T(8,128)(2,1)} %copy-done.3, ...), custom_call_target="tpu_custom_call" | custom-call | tf_op jit(solution)/shard_map/cross/pallas_call | solution.py:358
  122.5 1.9 %collective-permute-start.4 = (bf16[4,96,512]{2,1,0:T(8,128)(2,1)}, bf16[4,96,512]{2,1,0:T(8,128)(2,1)S(1)}, u32[]{:S(2)}, u32[]{:S(2)}) collective-permute-start(bf16[4,96,512]{2,1,0:T(8,128)(2,1)} %get-tuple-element.36), channel_id=1, source_target_pairs={{0,4},{4,8},{8,12},{12,16},{16,20},{20,24},{24,28},{28,32},{32,36}... | collective-permute-start | bytes 1179656 | tf_op jit(solution)/shard_map/ppermute | solution.py:522
  124.4 6.7 %collective-permute-start.5 = (bf16[4,96,512]{2,1,0:T(8,128)(2,1)}, bf16[4,96,512]{2,1,0:T(8,128)(2,1)S(1)}, u32[]{:S(2)}, u32[]{:S(2)}) collective-permute-start(bf16[4,96,512]{2,1,0:T(8,128)(2,1)} %get-tuple-element.37), channel_id=1, source_target_pairs={{4,0},{8,4},{12,8},{16,12},{20,16},{24,20},{28,24},{32,28},{36,32}... | collective-permute-start | bytes 1179656 | tf_op jit(solution)/shard_map/ppermute | solution.py:522
  131.1 1.4 add_convert_fusion.1
  132.8 2.8 %collective-permute-start.11 = (bf16[4,96,768]{2,1,0:T(8,128)(2,1)S(1)}, bf16[4,96,768]{2,1,0:T(8,128)(2,1)S(1)}, u32[]{:S(2)}, u32[]{:S(2)}) collective-permute-start(bf16[4,96,768]{2,1,0:T(8,128)(2,1)S(1)} %convert_select_fusion.3), channel_id=1, source_target_pairs={{0,2},{1,3},{2,0},{3,1},{4,6},{5,7},{6,4},{7,5},{8,10},{9,11},{10,... | collective-permute-start | bytes 1769480 | tf_op jit(solution)/shard_map/ppermute | solution.py:526
  136.2 2.8 %collective-permute-start.12 = (bf16[4,96,512]{2,1,0:T(8,128)(2,1)S(1)}, bf16[4,96,512]{2,1,0:T(8,128)(2,1)S(1)}, u32[]{:S(2)}, u32[]{:S(2)}) collective-permute-start(bf16[4,96,512]{2,1,0:T(8,128)(2,1)S(1)} %convert_select_fusion.5), channel_id=1, source_target_pairs={{0,2},{1,3},{2,0},{3,1},{4,6},{5,7},{6,4},{7,5},{8,10},{9,11},{10,... | collective-permute-start | bytes 1179656 | tf_op jit(solution)/shard_map/ppermute | solution.py:526
  139.2 12.2 %collective-permute-start.14 = (bf16[4,96,768]{2,1,0:T(8,128)(2,1)S(1)}, bf16[4,96,768]{2,1,0:T(8,128)(2,1)S(1)}, u32[]{:S(2)}, u32[]{:S(2)}) collective-permute-start(bf16[4,96,768]{2,1,0:T(8,128)(2,1)S(1)} %add_convert_fusion.1), channel_id=1, source_target_pairs={{0,1},{1,0},{2,3},{3,2},{4,5},{5,4},{6,7},{7,6},{8,9},{9,8},{10,11... | collective-permute-start | bytes 1769480 | tf_op jit(solution)/shard_map/ppermute | solution.py:526
  151.6 9.4 %collective-permute-start.15 = (bf16[4,96,768]{2,1,0:T(8,128)(2,1)S(1)}, bf16[4,96,768]{2,1,0:T(8,128)(2,1)S(1)}, u32[]{:S(2)}, u32[]{:S(2)}) collective-permute-start(bf16[4,96,768]{2,1,0:T(8,128)(2,1)S(1)} %add_convert_fusion.refs_4_), channel_id=1, source_target_pairs={{0,1},{1,0},{2,3},{3,2},{4,5},{5,4},{6,7},{7,6},{8,9},{9,8},{10,11... | collective-permute-start | bytes 1769480 | tf_op jit(solution)/shard_map/ppermute | solution.py:526
  161.1 4.0 %collective-permute-start.13 = (bf16[4,96,512]{2,1,0:T(8,128)(2,1)S(1)}, bf16[4,96,512]{2,1,0:T(8,128)(2,1)S(1)}, u32[]{:S(2)}, u32[]{:S(2)}) collective-permute-start(bf16[4,96,512]{2,1,0:T(8,128)(2,1)S(1)} %add_convert_fusion.2.mine_ref), channel_id=1, source_target_pairs={{0,1},{1,0},{2,3},{3,2},{4,5},{5,4},{6,7},{7,6},{8,9},{9,8},{10,11... | collective-permute-start | bytes 1179656 | tf_op jit(solution)/shard_map/ppermute | solution.py:526
  165.2 0.8 copy-done.10
  166.2 8.5 %early.1 = (f32[384,1024]{1,0:T(8,128)}, f32[384,1024]{1,0:T(8,128)}) custom-call(s32[8]{0:T(128)} %get-tuple-element.32.ordered_ref, bf16[4,96,768]{2,1,0:T(8,128)(2,1)} %copy-done.7, bf16[4,96,768]{2,1,0:T(8,128)(2,1)} %copy-done.10, bf16[3,1024,256]{2,1,0:T(8,128)(2,1)} %get-tuple-element.42.table_ref.refs_2_, ...), custom_call_target="tpu_custom_call" | custom-call | tf_op jit(solution)/shard_map/early/pallas_call | solution.py:445
  175.4 6.8 %last.1 = f32[4,96,2048]{2,1,0:T(8,128)} custom-call(s32[8]{0:T(128)} %get-tuple-element.32.ordered_ref, bf16[4,96,512]{2,1,0:T(8,128)(2,1)} %copy-done.9, bf16[4,96,512]{2,1,0:T(8,128)(2,1)} %copy-done.12, bf16[2,1024,256]{2,1,0:T(8,128)(2,1)} %get-tuple-element.34.table_ref.hi_ref, bf16[2,1024,256]{2,1,0:T(8,128)(2,1)} %get-tuple-element.54.lo_ref, ...), custom_call_target="tpu_custom_call" | custom-call | tf_op jit(solution)/shard_map/last/pallas_call | solution.py:495
  (60 shorter events, 6.7 us)
Async XLA Ops:
  8.6 25.1 %collective-permute-start.3 = (bf16[12,96,1024]{2,1,0:T(8,128)(2,1)}, bf16[12,96,1024]{2,1,0:T(8,128)(2,1)S(1)}, u32[]{:S(2)}, u32[]{:S(2)}) collective-permute-start(bf16[12,96,1024]{2,1,0:T(8,128)(2,1)} %normalize.3), channel_id=1, source_target_pairs={{0,1},{1,0},{2,3},{3,2},{4,5},{5,4},{6,7},{7,6},{8,9},{9,8},{10,11... | collective-permute-start | bytes 7077896 | tf_op jit(solution)/shard_map/ppermute | solution.py:526
  13.2 1.6 collective-permute-start
  14.9 14.4 %copy-start.3 = (bf16[4,32,1024]{2,1,0:T(8,128)(2,1)}, bf16[4,32,1024]{2,1,0:T(8,128)(2,1)S(1)}, u32[]{:S(2)}) copy-start(bf16[4,32,1024]{2,1,0:T(8,128)(2,1)S(1)} %constant_dynamic-update-slice_fusion.own_src_ref) | copy-start | bytes 786436
  14.9 17.8 %collective-permute-start.2 = (bf16[4,32,1024]{2,1,0:T(8,128)(2,1)S(1)}, bf16[4,32,1024]{2,1,0:T(8,128)(2,1)S(1)}, u32[]{:S(2)}, u32[]{:S(2)}) collective-permute-start(bf16[4,32,1024]{2,1,0:T(8,128)(2,1)S(1)} %constant_dynamic-update-slice_fusion.own_src_ref), channel_id=1, source_target_pairs={{0,4},{4,8},{8,12},{12,16},{16,20},{20,24},{24,28},{28,32},{32,36}... | collective-permute-start | bytes 786440 | tf_op jit(solution)/shard_map/ppermute | solution.py:522
  18.1 14.8 %collective-permute-start.1 = (bf16[4,32,1024]{2,1,0:T(8,128)(2,1)S(1)}, bf16[4,32,1024]{2,1,0:T(8,128)(2,1)S(1)}, u32[]{:S(2)}, u32[]{:S(2)}) collective-permute-start(bf16[4,32,1024]{2,1,0:T(8,128)(2,1)S(1)} %constant_dynamic-update-slice_fusion.own_src_ref), channel_id=1, source_target_pairs={{4,0},{8,4},{12,8},{16,12},{20,16},{24,20},{28,24},{32,28},{36,32}... | collective-permute-start | bytes 786440 | tf_op jit(solution)/shard_map/ppermute | solution.py:522
  32.7 1.0 copy-start.5
  32.9 0.9 copy-start.6
  33.8 1.4 copy-start
  35.2 23.7 %copy-start.13 = (s32[8]{0:T(128)S(1)}, s32[8]{0:T(128)}, u32[]{:S(2)}) copy-start(s32[8]{0:T(128)} %get-tuple-element.32.ordered_ref) | copy-start | bytes 100
  53.3 14.9 %collective-permute-start.8 = (bf16[4,96,768]{2,1,0:T(8,128)(2,1)}, bf16[4,96,768]{2,1,0:T(8,128)(2,1)S(1)}, u32[]{:S(2)}, u32[]{:S(2)}) collective-permute-start(bf16[4,96,768]{2,1,0:T(8,128)(2,1)} %get-tuple-element.44), channel_id=1, source_target_pairs={{4,0},{8,4},{12,8},{16,12},{20,16},{24,20},{28,24},{32,28},{36,32}... | collective-permute-start | bytes 1769480 | tf_op jit(solution)/shard_map/ppermute | solution.py:522
  56.9 17.4 %collective-permute-start.9 = (bf16[4,96,768]{2,1,0:T(8,128)(2,1)}, bf16[4,96,768]{2,1,0:T(8,128)(2,1)S(1)}, u32[]{:S(2)}, u32[]{:S(2)}) collective-permute-start(bf16[4,96,768]{2,1,0:T(8,128)(2,1)} %get-tuple-element.45), channel_id=1, source_target_pairs={{0,4},{4,8},{8,12},{12,16},{16,20},{20,24},{24,28},{28,32},{32,36}... | collective-permute-start | bytes 1769480 | tf_op jit(solution)/shard_map/ppermute | solution.py:522
  76.6 54.5 %collective-permute-start.10 = (bf16[4,96,768]{2,1,0:T(8,128)(2,1)}, bf16[4,96,768]{2,1,0:T(8,128)(2,1)}, u32[]{:S(2)}, u32[]{:S(2)}) collective-permute-start(bf16[4,96,768]{2,1,0:T(8,128)(2,1)} %convert_select_fusion.4), channel_id=1, source_target_pairs={{0,2},{1,3},{2,0},{3,1},{4,6},{5,7},{6,4},{7,5},{8,10},{9,11},{10,... | collective-permute-start | bytes 1769480 | tf_op jit(solution)/shard_map/ppermute | solution.py:526
  98.3 34.3 %collective-permute-start.6 = (bf16[4,96,768]{2,1,0:T(8,128)(2,1)}, bf16[4,96,768]{2,1,0:T(8,128)(2,1)S(1)}, u32[]{:S(2)}, u32[]{:S(2)}) collective-permute-start(bf16[4,96,768]{2,1,0:T(8,128)(2,1)} %get-tuple-element.40), channel_id=1, source_target_pairs={{0,4},{4,8},{8,12},{12,16},{16,20},{20,24},{24,28},{28,32},{32,36}... | collective-permute-start | bytes 1769480 | tf_op jit(solution)/shard_map/ppermute | solution.py:522
  100.2 32.4 %collective-permute-start.7 = (bf16[4,96,768]{2,1,0:T(8,128)(2,1)}, bf16[4,96,768]{2,1,0:T(8,128)(2,1)S(1)}, u32[]{:S(2)}, u32[]{:S(2)}) collective-permute-start(bf16[4,96,768]{2,1,0:T(8,128)(2,1)} %get-tuple-element.41), channel_id=1, source_target_pairs={{4,0},{8,4},{12,8},{16,12},{20,16},{24,20},{28,24},{32,28},{36,32}... | collective-permute-start | bytes 1769480 | tf_op jit(solution)/shard_map/ppermute | solution.py:522
  109.1 22.0 %copy-start.1 = (f32[4,96,768]{2,1,0:T(8,128)S(1)}, f32[4,96,768]{2,1,0:T(8,128)}, u32[]{:S(2)}) copy-start(f32[4,96,768]{2,1,0:T(8,128)} %get-tuple-element.43) | copy-start | bytes 3538948
  122.5 13.5 %collective-permute-start.4 = (bf16[4,96,512]{2,1,0:T(8,128)(2,1)}, bf16[4,96,512]{2,1,0:T(8,128)(2,1)S(1)}, u32[]{:S(2)}, u32[]{:S(2)}) collective-permute-start(bf16[4,96,512]{2,1,0:T(8,128)(2,1)} %get-tuple-element.36), channel_id=1, source_target_pairs={{0,4},{4,8},{8,12},{12,16},{16,20},{20,24},{24,28},{28,32},{32,36}... | collective-permute-start | bytes 1179656 | tf_op jit(solution)/shard_map/ppermute | solution.py:522
  124.4 8.2 %copy-start.2 = (f32[4,96,768]{2,1,0:T(8,128)S(1)}, f32[4,96,768]{2,1,0:T(8,128)}, u32[]{:S(2)}) copy-start(f32[4,96,768]{2,1,0:T(8,128)} %get-tuple-element.46) | copy-start | bytes 3538948
  124.4 11.6 %collective-permute-start.5 = (bf16[4,96,512]{2,1,0:T(8,128)(2,1)}, bf16[4,96,512]{2,1,0:T(8,128)(2,1)S(1)}, u32[]{:S(2)}, u32[]{:S(2)}) collective-permute-start(bf16[4,96,512]{2,1,0:T(8,128)(2,1)} %get-tuple-element.37), channel_id=1, source_target_pairs={{4,0},{8,4},{12,8},{16,12},{20,16},{24,20},{28,24},{32,28},{36,32}... | collective-permute-start | bytes 1179656 | tf_op jit(solution)/shard_map/ppermute | solution.py:522
  132.5 6.7 %copy-start.7 = (bf16[4,96,768]{2,1,0:T(8,128)(2,1)}, bf16[4,96,768]{2,1,0:T(8,128)(2,1)S(1)}, u32[]{:S(2)}) copy-start(bf16[4,96,768]{2,1,0:T(8,128)(2,1)S(1)} %add_convert_fusion.1) | copy-start | bytes 1769476
  132.8 3.2 %copy-start.4 = (f32[4,96,512]{2,1,0:T(8,128)S(1)}, f32[4,96,512]{2,1,0:T(8,128)}, u32[]{:S(2)}) copy-start(f32[4,96,512]{2,1,0:T(8,128)} %get-tuple-element.49) | copy-start | bytes 2359300
  132.8 18.6 %collective-permute-start.11 = (bf16[4,96,768]{2,1,0:T(8,128)(2,1)S(1)}, bf16[4,96,768]{2,1,0:T(8,128)(2,1)S(1)}, u32[]{:S(2)}, u32[]{:S(2)}) collective-permute-start(bf16[4,96,768]{2,1,0:T(8,128)(2,1)S(1)} %convert_select_fusion.3), channel_id=1, source_target_pairs={{0,2},{1,3},{2,0},{3,1},{4,6},{5,7},{6,4},{7,5},{8,10},{9,11},{10,... | collective-permute-start | bytes 1769480 | tf_op jit(solution)/shard_map/ppermute | solution.py:526
  136.2 24.8 %collective-permute-start.12 = (bf16[4,96,512]{2,1,0:T(8,128)(2,1)S(1)}, bf16[4,96,512]{2,1,0:T(8,128)(2,1)S(1)}, u32[]{:S(2)}, u32[]{:S(2)}) collective-permute-start(bf16[4,96,512]{2,1,0:T(8,128)(2,1)S(1)} %convert_select_fusion.5), channel_id=1, source_target_pairs={{0,2},{1,3},{2,0},{3,1},{4,6},{5,7},{6,4},{7,5},{8,10},{9,11},{10,... | collective-permute-start | bytes 1179656 | tf_op jit(solution)/shard_map/ppermute | solution.py:526
  139.2 26.0 %collective-permute-start.14 = (bf16[4,96,768]{2,1,0:T(8,128)(2,1)S(1)}, bf16[4,96,768]{2,1,0:T(8,128)(2,1)S(1)}, u32[]{:S(2)}, u32[]{:S(2)}) collective-permute-start(bf16[4,96,768]{2,1,0:T(8,128)(2,1)S(1)} %add_convert_fusion.1), channel_id=1, source_target_pairs={{0,1},{1,0},{2,3},{3,2},{4,5},{5,4},{6,7},{7,6},{8,9},{9,8},{10,11... | collective-permute-start | bytes 1769480 | tf_op jit(solution)/shard_map/ppermute | solution.py:526
  151.6 13.6 %copy-start.8 = (bf16[4,96,768]{2,1,0:T(8,128)(2,1)}, bf16[4,96,768]{2,1,0:T(8,128)(2,1)S(1)}, u32[]{:S(2)}) copy-start(bf16[4,96,768]{2,1,0:T(8,128)(2,1)S(1)} %add_convert_fusion.refs_4_) | copy-start | bytes 1769476
  151.6 13.6 %collective-permute-start.15 = (bf16[4,96,768]{2,1,0:T(8,128)(2,1)S(1)}, bf16[4,96,768]{2,1,0:T(8,128)(2,1)S(1)}, u32[]{:S(2)}, u32[]{:S(2)}) collective-permute-start(bf16[4,96,768]{2,1,0:T(8,128)(2,1)S(1)} %add_convert_fusion.refs_4_), channel_id=1, source_target_pairs={{0,1},{1,0},{2,3},{3,2},{4,5},{5,4},{6,7},{7,6},{8,9},{9,8},{10,11... | collective-permute-start | bytes 1769480 | tf_op jit(solution)/shard_map/ppermute | solution.py:526
  161.1 13.5 %copy-start.9 = (bf16[4,96,512]{2,1,0:T(8,128)(2,1)}, bf16[4,96,512]{2,1,0:T(8,128)(2,1)S(1)}, u32[]{:S(2)}) copy-start(bf16[4,96,512]{2,1,0:T(8,128)(2,1)S(1)} %add_convert_fusion.2.mine_ref) | copy-start | bytes 1179652
  161.1 13.5 %collective-permute-start.13 = (bf16[4,96,512]{2,1,0:T(8,128)(2,1)S(1)}, bf16[4,96,512]{2,1,0:T(8,128)(2,1)S(1)}, u32[]{:S(2)}, u32[]{:S(2)}) collective-permute-start(bf16[4,96,512]{2,1,0:T(8,128)(2,1)S(1)} %add_convert_fusion.2.mine_ref), channel_id=1, source_target_pairs={{0,1},{1,0},{2,3},{3,2},{4,5},{5,4},{6,7},{7,6},{8,9},{9,8},{10,11... | collective-permute-start | bytes 1179656 | tf_op jit(solution)/shard_map/ppermute | solution.py:526
  165.2 0.8 copy-start.10
  165.2 1.0 copy-start.11
  174.7 0.7 copy-start.12
